TPU v7x, 32 devices: a whole 2x2x4 slice. The times are simulated.
32 devices in a mesh: fsdp: 32 (over z, y, x, core).
Axes of the slice: x: 2, y: 2, z: 4, core: 2. Of those that a mesh axis runs over, the one named last changes fastest.
Arguments:
- block_in: bfloat16 [12608, 768], P('fsdp'), may hold values from -6 to 6
- out_cotangent: bfloat16 [12608, 768], P('fsdp'), may hold values from -6 to 6
- expert_routes: int32 [12608, 2], P('fsdp'), may hold values from 0 to 31, all different within a row; in each aligned block of 197 rows (0 to 196, 197 to 393, ...) at most 16 rows name the same one
- ln1_gain: bfloat16 [768], P('fsdp'), may hold values from 0.5 to 1.5
- ln1_shift: bfloat16 [768], P('fsdp'), may hold values from -1.75 to 1.75
- w_qkv: bfloat16 [768, 2304], P('fsdp'), may hold values from -0.21875 to 0.21875
- bias_query: bfloat16 [768], P('fsdp'), may hold values from -3 to 3
- bias_value: bfloat16 [768], P('fsdp'), may hold values from -3 to 3
- w_out: bfloat16 [768, 768], P(None, 'fsdp'), may hold values from -0.875 to 0.875
- bias_out: bfloat16 [768], P('fsdp'), may hold values from -3 to 3
- ln2_gain: bfloat16 [768], P('fsdp'), may hold values from 0.5 to 1.5
- ln2_shift: bfloat16 [768], P('fsdp'), may hold values from -1.75 to 1.75
- w_router: bfloat16 [768, 32], P('fsdp'), may hold values from -0.21875 to 0.21875
- expert_bias: bfloat16 [32, 768], P(None, 'fsdp'), may hold values from -12 to 12
- w_expert_in: bfloat16 [98304, 768], P('fsdp'), may hold values from -0.21875 to 0.21875
- bias_hidden: float32 [98304], P('fsdp'), may hold values from -3 to 3
- w_expert_out: bfloat16 [98304, 768], P('fsdp'), may hold values from -0.875 to 0.875
Outputs:
- block_out: float32 [12608, 768], P('fsdp')
- input_grad: float32 [12608, 768], P('fsdp')
- grad_ln1_gain: float32 [768], P('fsdp')
- grad_ln1_shift: float32 [768], P('fsdp')
- grad_w_qkv: float32 [768, 2304], P('fsdp')
- grad_bias_query: float32 [768], P('fsdp')
- grad_bias_value: float32 [768], P('fsdp')
- grad_w_out: float32 [768, 768], P(None, 'fsdp')
- grad_bias_out: float32 [768], P('fsdp')
- grad_ln2_gain: float32 [768], P('fsdp')
- grad_ln2_shift: float32 [768], P('fsdp')
- grad_w_router: float32 [768, 32], P('fsdp')
- grad_expert_bias: float32 [32, 768], P(None, 'fsdp')
- grad_w_expert_in: float32 [98304, 768], P('fsdp')
- grad_bias_hidden: float32 [98304], P('fsdp')
- grad_w_expert_out: float32 [98304, 768], P('fsdp')
Inputs may be any that keep to these rules, and one draw needn't show every extreme that they name: `expert_routes`: each row names two different experts. Within each image (aligned blocks of 197 rows), no expert is named by more than 16 tokens, a bound that some block reaches.
All inputs are finite; a program needn't handle non-finite values.
Results may differ from a plain program's by a relative error of at most 0.015.
Values may be sent and summed in bfloat16 or wider, within the bound.
No kernel may reach another device: no remote copies, remote signals or barrier semaphores. Data moves between devices by JAX's collectives and lax.ppermute only.
A program may use at most 256 MiB of HBM per device.

v0:
```python
import math

import jax
import jax.numpy as jnp
from jax import lax
from jax.sharding import PartitionSpec as P

D = 768
HEADS = 12
HEAD_DIM = 64
E = 32
SEQ = 197
CAP = 16


epsilon = 1e-06
highest = lax.Precision.HIGHEST


def normalize(values):
    centered = values - jnp.mean(values, axis=-1, keepdims=True)
    inverse = lax.rsqrt(jnp.mean(centered * centered, axis=-1, keepdims=True) + epsilon)
    return (centered * inverse, inverse)


def norm_back(upstream, normed, inverse):
    return inverse * (
        upstream
        - jnp.mean(upstream, axis=-1, keepdims=True)
        - normed * jnp.mean(upstream * normed, axis=-1, keepdims=True)
    )


def gelu_slope(values):
    cumulative = 0.5 * (1.0 + lax.erf(values * (1.0 / math.sqrt(2.0))))
    density = jnp.exp(-0.5 * values * values) * (1.0 / math.sqrt(2.0 * math.pi))
    return cumulative + values * density


def slot_numbers(route_pairs):
    ordered = jnp.concatenate([route_pairs[:, :, 0], route_pairs[:, :, 1]], axis=1)
    matched = (ordered[:, :, None] == jnp.arange(E, dtype=jnp.int32)).astype(jnp.int32)
    earlier = jnp.cumsum(matched, axis=1) - matched
    position = jnp.sum(earlier * matched, axis=-1)
    return jnp.stack([position[:, :SEQ], position[:, SEQ:]], axis=-1)


def take_rows(source_rows, positions):
    return jax.vmap(lambda table_rows, index_rows: jnp.take(table_rows, index_rows, axis=0))(
        source_rows, positions
    )


def to_owners(slot_rows, owners):
    group_size = slot_rows.shape[0]
    spread = jnp.broadcast_to(
        slot_rows.reshape(group_size, E, 1, CAP, D), (group_size, E, owners, CAP, D)
    )
    return spread.reshape(group_size, E * owners, CAP, D)


def on_device(
    block_in,
    out_cotangent,
    expert_routes,
    ln1_gain,
    ln1_shift,
    w_qkv,
    bias_query,
    bias_value,
    w_out,
    bias_out,
    ln2_gain,
    ln2_shift,
    w_router,
    expert_bias,
    w_expert_in,
    bias_hidden,
    w_expert_out,
):
    images = block_in.shape[0] // SEQ
    owners = lax.axis_size("fsdp") // E
    hidden_local = w_expert_in.shape[0]
    slots_all = E * CAP
    score_scale = 1.0 / math.sqrt(HEAD_DIM)
    (
        gain_half,
        shift_half,
        qkv_full,
        query_half,
        value_half,
        out_full,
        out_half,
        gain_two_half,
        shift_two_half,
        router_full,
        slot_half,
    ) = (
        lax.all_gather(ln1_gain, "fsdp", axis=0, tiled=True),
        lax.all_gather(ln1_shift, "fsdp", axis=0, tiled=True),
        lax.all_gather(w_qkv, "fsdp", axis=0, tiled=True),
        lax.all_gather(bias_query, "fsdp", axis=0, tiled=True),
        lax.all_gather(bias_value, "fsdp", axis=0, tiled=True),
        lax.all_gather(w_out, "fsdp", axis=1, tiled=True),
        lax.all_gather(bias_out, "fsdp", axis=0, tiled=True),
        lax.all_gather(ln2_gain, "fsdp", axis=0, tiled=True),
        lax.all_gather(ln2_shift, "fsdp", axis=0, tiled=True),
        lax.all_gather(w_router, "fsdp", axis=0, tiled=True),
        lax.all_gather(expert_bias, "fsdp", axis=1, tiled=True),
    )
    gain_one = gain_half.astype(jnp.float32)
    shift_one = shift_half.astype(jnp.float32)
    gain_two = gain_two_half.astype(jnp.float32)
    shift_two = shift_two_half.astype(jnp.float32)
    slot_bias = slot_half.astype(jnp.float32)
    inputs = block_in.reshape(images, SEQ, D).astype(jnp.float32)
    first_hat, first_rstd = normalize(inputs)
    first_norm = (first_hat * gain_one + shift_one).astype(jnp.bfloat16)
    projected = jnp.einsum("psd,de->pse", first_norm, qkv_full, preferred_element_type=jnp.float32)
    queries = (
        (projected[..., :D] + query_half.astype(jnp.float32))
        .astype(jnp.bfloat16)
        .reshape(images, SEQ, HEADS, HEAD_DIM)
    )
    key_rows = projected[..., D : 2 * D].astype(jnp.bfloat16).reshape(images, SEQ, HEADS, HEAD_DIM)
    values = (
        (projected[..., 2 * D :] + value_half.astype(jnp.float32))
        .astype(jnp.bfloat16)
        .reshape(images, SEQ, HEADS, HEAD_DIM)
    )
    scores = (
        jnp.einsum("pqhc,pkhc->phqk", queries, key_rows, preferred_element_type=jnp.float32)
        * score_scale
    )
    raised = jnp.exp(scores)
    totals = jnp.sum(raised, axis=-1, keepdims=True)
    log_total = jnp.log(totals)
    attend = (raised / totals).astype(jnp.bfloat16)
    context = (
        jnp.einsum("phqk,pkhc->pqhc", attend, values, preferred_element_type=jnp.float32)
        .astype(jnp.bfloat16)
        .reshape(images, SEQ, D)
    )
    residual = (
        inputs
        + jnp.einsum("psd,de->pse", context, out_full, preferred_element_type=jnp.float32)
        + out_half.astype(jnp.float32)
    )
    second_hat, second_rstd = normalize(residual)
    second_norm = (second_hat * gain_two + shift_two).astype(jnp.bfloat16)
    logits = jnp.einsum("psd,de->pse", second_norm, router_full, preferred_element_type=jnp.float32)
    raised_logits = jnp.exp(logits)
    router_prob = raised_logits / jnp.sum(raised_logits, axis=-1, keepdims=True)
    route_pairs = expert_routes.reshape(images, SEQ, 2)
    gate_values = jnp.take_along_axis(router_prob, route_pairs, axis=-1)
    placed = route_pairs * CAP + slot_numbers(route_pairs)
    columns = jnp.arange(slots_all, dtype=jnp.int32)
    matches = (placed[..., None] == columns).astype(jnp.float32)
    dispatch = jnp.sum(matches, axis=2).astype(jnp.bfloat16)
    weighted = jnp.sum(matches * gate_values[..., None], axis=2)
    per_group = 1
    groups = images // per_group

    def regroup(stacked):
        return stacked.reshape((groups, per_group) + stacked.shape[1:])

    def run_experts(arrived):
        rows = arrived.reshape(-1, D)
        before_act = (
            lax.dot_general(
                rows, w_expert_in, (((1,), (1,)), ((), ())), preferred_element_type=jnp.float32
            )
            + bias_hidden
        )
        activated = jax.nn.gelu(before_act, approximate=False).astype(jnp.bfloat16)
        partial_out = jnp.dot(activated, w_expert_out, preferred_element_type=jnp.float32).astype(
            jnp.bfloat16
        )
        returned = lax.all_to_all(
            partial_out.reshape(arrived.shape), "fsdp", split_axis=1, concat_axis=1, tiled=True
        )
        kept_shape = arrived.shape[:-1] + (hidden_local,)
        return (returned, arrived, before_act.reshape(kept_shape), activated.reshape(kept_shape))

    def forward_group(unused_in, group_in):
        normed_part, dispatch_part = group_in
        filled = jnp.einsum(
            "psn,psd->pnd", dispatch_part, normed_part, preferred_element_type=jnp.float32
        ).astype(jnp.bfloat16)
        outgoing = to_owners(filled, owners)
        returned, arrived, before_act, activated = run_experts(
            lax.all_to_all(outgoing, "fsdp", split_axis=1, concat_axis=1, tiled=True)
        )
        summed = (
            jnp.sum(returned.reshape(per_group, E, owners, CAP, D).astype(jnp.float32), axis=2)
            + slot_bias[None, :, None, :]
        )
        return (
            unused_in,
            (summed.reshape(per_group, slots_all, D), arrived, before_act, activated),
        )

    unused_out, (expert_rows, arrived_all, before_all, activated_all) = lax.scan(
        forward_group, jnp.zeros((), jnp.float32), (regroup(second_norm), regroup(dispatch))
    )
    expert_rows = expert_rows.reshape(images, slots_all, D)
    flat_place = placed.reshape(images, SEQ * 2)
    picked = take_rows(expert_rows, flat_place).reshape(images, SEQ, 2, D)
    block_out = residual + jnp.sum(picked * gate_values[..., None], axis=2)
    upstream = out_cotangent.reshape(images, SEQ, D).astype(jnp.float32)
    gate_grad = jnp.sum(picked * upstream[:, :, None, :], axis=-1)
    slot_cot = jnp.einsum("psn,psd->pnd", weighted, upstream, precision=highest)
    grad_slot_bias = jnp.sum(slot_cot.reshape(images, E, CAP, D), axis=(0, 2))
    slot_cot_half = slot_cot.astype(jnp.bfloat16)

    def backward_group(running, group_in):
        grad_in_w, grad_in_b, grad_out_w = running
        cot_part, arrived, before_act, activated = group_in
        cot_arrived = lax.all_to_all(
            to_owners(cot_part, owners), "fsdp", split_axis=1, concat_axis=1, tiled=True
        )
        cot_rows = cot_arrived.reshape(-1, D)
        token_rows = arrived.reshape(-1, D)
        before_rows = before_act.reshape(-1, hidden_local)
        hidden_rows = activated.reshape(-1, hidden_local)
        grad_out_w = grad_out_w + lax.dot_general(
            hidden_rows, cot_rows, (((0,), (0,)), ((), ())), preferred_element_type=jnp.float32
        )
        hidden_grad = lax.dot_general(
            cot_rows, w_expert_out, (((1,), (1,)), ((), ())), preferred_element_type=jnp.float32
        )
        before_grad = hidden_grad * gelu_slope(before_rows)
        grad_in_b = grad_in_b + jnp.sum(before_grad, axis=0)
        before_half = before_grad.astype(jnp.bfloat16)
        grad_in_w = grad_in_w + lax.dot_general(
            before_half, token_rows, (((0,), (0,)), ((), ())), preferred_element_type=jnp.float32
        )
        partial_in = (
            jnp.dot(before_half, w_expert_in, preferred_element_type=jnp.float32)
            .astype(jnp.bfloat16)
            .reshape(cot_arrived.shape)
        )
        returned = lax.all_to_all(partial_in, "fsdp", split_axis=1, concat_axis=1, tiled=True)
        summed = jnp.sum(returned.reshape(per_group, E, owners, CAP, D).astype(jnp.float32), axis=2)
        return ((grad_in_w, grad_in_b, grad_out_w), summed.reshape(per_group, slots_all, D))

    zero_rows = jnp.zeros(w_expert_in.shape, jnp.float32)
    (grad_w_expert_in, grad_bias_hidden, grad_w_expert_out), slot_grad = lax.scan(
        backward_group,
        (zero_rows, jnp.zeros(bias_hidden.shape, jnp.float32), zero_rows),
        (regroup(slot_cot_half), arrived_all, before_all, activated_all),
    )
    slot_grad = slot_grad.reshape(images, slots_all, D)
    moe_grad = jnp.sum(take_rows(slot_grad, flat_place).reshape(images, SEQ, 2, D), axis=2)
    prob_grad = jnp.sum(
        gate_grad[..., None]
        * (route_pairs[..., None] == jnp.arange(E, dtype=jnp.int32)).astype(jnp.float32),
        axis=2,
    )
    logit_grad = router_prob * (
        prob_grad - jnp.sum(prob_grad * router_prob, axis=-1, keepdims=True)
    )
    logit_half = logit_grad.astype(jnp.bfloat16)
    grad_router = jnp.einsum(
        "psd,pse->de", second_norm, logit_half, preferred_element_type=jnp.float32
    )
    second_grad = moe_grad + jnp.einsum(
        "pse,de->psd", logit_half, router_full, preferred_element_type=jnp.float32
    )
    grad_gain_two = jnp.sum(second_grad * second_hat, axis=(0, 1))
    grad_shift_two = jnp.sum(second_grad, axis=(0, 1))
    residual_grad = upstream + norm_back(second_grad * gain_two, second_hat, second_rstd)
    grad_out_bias = jnp.sum(residual_grad, axis=(0, 1))
    residual_half = residual_grad.astype(jnp.bfloat16)
    grad_out = jnp.einsum("psd,pse->de", context, residual_half, preferred_element_type=jnp.float32)
    context_grad = (
        jnp.einsum("pse,de->psd", residual_half, out_full, preferred_element_type=jnp.float32)
        .astype(jnp.bfloat16)
        .reshape(images, SEQ, HEADS, HEAD_DIM)
    )
    scores_again = (
        jnp.einsum("pqhc,pkhc->phqk", queries, key_rows, preferred_element_type=jnp.float32)
        * score_scale
    )
    prob_again = jnp.exp(scores_again - log_total)
    prob_half = prob_again.astype(jnp.bfloat16)
    value_grad = jnp.einsum(
        "phqk,pqhc->pkhc", prob_half, context_grad, preferred_element_type=jnp.float32
    )
    dprob = jnp.einsum("pqhc,pkhc->phqk", context_grad, values, preferred_element_type=jnp.float32)
    row_dot = jnp.sum(prob_again * dprob, axis=-1, keepdims=True)
    score_grad = (prob_again * (dprob - row_dot) * score_scale).astype(jnp.bfloat16)
    query_grad = jnp.einsum(
        "phqk,pkhc->pqhc", score_grad, key_rows, preferred_element_type=jnp.float32
    )
    key_grad = jnp.einsum(
        "phqk,pqhc->pkhc", score_grad, queries, preferred_element_type=jnp.float32
    )
    grad_query_bias = jnp.sum(query_grad, axis=(0, 1)).reshape(D)
    grad_value_bias = jnp.sum(value_grad, axis=(0, 1)).reshape(D)
    proj_half = jnp.concatenate(
        [
            query_grad.reshape(images, SEQ, D),
            key_grad.reshape(images, SEQ, D),
            value_grad.reshape(images, SEQ, D),
        ],
        axis=-1,
    ).astype(jnp.bfloat16)
    grad_qkv = jnp.einsum("psd,pse->de", first_norm, proj_half, preferred_element_type=jnp.float32)
    first_grad = jnp.einsum("pse,de->psd", proj_half, qkv_full, preferred_element_type=jnp.float32)
    grad_gain_one = jnp.sum(first_grad * first_hat, axis=(0, 1))
    grad_shift_one = jnp.sum(first_grad, axis=(0, 1))
    input_grad = residual_grad + norm_back(first_grad * gain_one, first_hat, first_rstd)
    (
        grad_ln1_gain,
        grad_ln1_shift,
        grad_w_qkv,
        grad_bias_query,
        grad_bias_value,
        grad_w_out,
        grad_bias_out,
        grad_ln2_gain,
        grad_ln2_shift,
        grad_w_router,
        grad_expert_bias,
    ) = (
        lax.psum_scatter(grad_gain_one, "fsdp", scatter_dimension=0, tiled=True),
        lax.psum_scatter(grad_shift_one, "fsdp", scatter_dimension=0, tiled=True),
        lax.psum_scatter(grad_qkv, "fsdp", scatter_dimension=0, tiled=True),
        lax.psum_scatter(grad_query_bias, "fsdp", scatter_dimension=0, tiled=True),
        lax.psum_scatter(grad_value_bias, "fsdp", scatter_dimension=0, tiled=True),
        lax.psum_scatter(grad_out, "fsdp", scatter_dimension=1, tiled=True),
        lax.psum_scatter(grad_out_bias, "fsdp", scatter_dimension=0, tiled=True),
        lax.psum_scatter(grad_gain_two, "fsdp", scatter_dimension=0, tiled=True),
        lax.psum_scatter(grad_shift_two, "fsdp", scatter_dimension=0, tiled=True),
        lax.psum_scatter(grad_router, "fsdp", scatter_dimension=0, tiled=True),
        lax.psum_scatter(grad_slot_bias, "fsdp", scatter_dimension=1, tiled=True),
    )
    return (
        block_out.reshape(images * SEQ, D),
        input_grad.reshape(images * SEQ, D),
        grad_ln1_gain,
        grad_ln1_shift,
        grad_w_qkv,
        grad_bias_query,
        grad_bias_value,
        grad_w_out,
        grad_bias_out,
        grad_ln2_gain,
        grad_ln2_shift,
        grad_w_router,
        grad_expert_bias,
        grad_w_expert_in,
        grad_bias_hidden,
        grad_w_expert_out,
    )


def solution(mesh):
    in_specs = (
        P("fsdp", None),
        P("fsdp", None),
        P("fsdp", None),
        P("fsdp"),
        P("fsdp"),
        P("fsdp", None),
        P("fsdp"),
        P("fsdp"),
        P(None, "fsdp"),
        P("fsdp"),
        P("fsdp"),
        P("fsdp"),
        P("fsdp", None),
        P(None, "fsdp"),
        P("fsdp", None),
        P("fsdp"),
        P("fsdp", None),
    )
    out_specs = (
        P("fsdp", None),
        P("fsdp", None),
        P("fsdp"),
        P("fsdp"),
        P("fsdp", None),
        P("fsdp"),
        P("fsdp"),
        P(None, "fsdp"),
        P("fsdp"),
        P("fsdp"),
        P("fsdp"),
        P("fsdp", None),
        P(None, "fsdp"),
        P("fsdp", None),
        P("fsdp"),
        P("fsdp", None),
    )
    return jax.shard_map(
        on_device, mesh=mesh, in_specs=in_specs, out_specs=out_specs, check_vma=False
    )
```

profile of v0, /device:TPU:0, one launch (start us, length us, event | category | flops | bytes accessed | tf_op | source)
XLA Modules:
  0.0 972.5 jit_solution(10148377917007443124)
XLA Ops:
  20.3 42.7 %all-reduce.18 = (bf16[768]{0:T(1024)(128)(2,1)S(1)}, bf16[768]{0:T(1024)(128)(2,1)S(1)}, bf16[768]{0:T(1024)(128)(2,1)S(1)}, bf16[768]{0:T(1024)(128)(2,1)S(1)}...) all-reduce(bf16[768]{0:T(1024)(128)(2,1)S(1)} %dynamic-update-slice, ...), channel_id=1, replica_groups=mesh['fsdp'=32] {'fsdp'}, use_global_device_ids=true, to_apply=%add.2 | all-reduce | flops 5376 | bytes 21504
  64.1 40.7 %all_gather.42 = bf16[32,768]{0,1:T(8,128)(2,1)S(1)} all-gather(bf16[32,24]{0,1:T(8,128)(2,1)S(1)} %copy-done.56), channel_id=1, replica_groups=mesh['fsdp'=32] {'fsdp'}, dimensions={1}, use_global_device_ids=true | all-gather | bytes 50688 | tf_op jit(solution)/shard_map/all_gather | solution.py:109
  107.9 40.2 %all_gather.43 = bf16[768,32]{1,0:T(8,128)(2,1)} all-gather(bf16[24,32]{1,0:T(8,128)(2,1)S(1)} %copy-done.57), channel_id=1, replica_groups=mesh['fsdp'=32] {'fsdp'}, dimensions={0}, use_global_device_ids=true | all-gather | bytes 50688 | tf_op jit(solution)/shard_map/all_gather | solution.py:108
  168.9 13.7 %gather_fusion = f32[788]{0:T(1024)S(1)} fusion(f32[2,197,32]{1,2,0:T(8,128)S(1)} %fusion.77, s32[788]{0:T(1024)S(1)} %reshape.404), kind=kCustom, calls=%fused_computation.2 | custom fusion | bytes 15760 | tf_op jit(solution)/shard_map/jit(take_along_axis)/gather | solution.py:155
  183.8 10.1 %select_reduce_fusion = (f32[2,197,512]{2,1,0:T(8,128)S(1)}, bf16[2,197,512]{2,1,0:T(8,128)(2,1)S(1)}) fusion(f32[2,197,2]{2,1,0:T(8,128)S(1)} %copy.179, s32[2,197,2]{2,1,0:T(8,128)S(1)} %copy-done.33), kind=kLoop, calls=%fused_computation.85 | loop fusion | flops 1613824 | bytes 1216672 | tf_op jit(solution)/shard_map/reduce_sum | solution.py:160
  198.3 145.3 %while.33 = (s32[]{:T(128)}, f32[2,1,512,768]{3,2,1,0:T(8,128)S(1)}, bf16[2,1,32,16,768]{4,3,2,1,0:T(8,128)(2,1)}, f32[2,1,32,16,3072]{4,3,2,1,0:T(8,128)}, bf16...) while((s32[]{:T(128)}, ...), condition=%wide.region_10.11_spmd, body=%wide.region_9.10_spmd.sunk | while | flops 5092147200 | bytes 109937976 | solution.py:203
  200.0 22.5 %all_to_all.26 = bf16[1,32,16,768]{3,2,0,1:T(8,128)(2,1)S(1)} all-to-all(bf16[1,32,16,768]{3,2,0,1:T(8,128)(2,1)S(1)} %bitcast.226), channel_id=1, replica_groups=mesh['fsdp'=32] {'fsdp'}, dimensions={1} | all-to-all | bytes 1572864 | tf_op jit(solution)/shard_map/while/body/eval_jaxpr/all_to_all | solution.py:192
  222.5 18.4 %fusion.149 = (bf16[512,3072]{1,0:T(8,128)(2,1)S(1)}, f32[512,3072]{1,0:T(8,128)}) fusion(f32[3072]{0:T(1024)} %get-tuple-element.567, bf16[512,768]{1,0:T(8,128)(2,1)S(1)} %bitcast.224, bf16[3072,768]{1,0:T(8,128)(2,1)} %get-tuple-element.566), kind=kOutput, calls=%fused_computation.6.clone.1 | convolution fusion | flops 2519728128 | bytes 14954496 | tf_op jit(solution)/shard_map/while/body/eval_jaxpr/dot_general | solution.py:170
  258.1 10.8 %all-to-all-done.1 = bf16[1,32,16,768]{3,2,0,1:T(8,128)(2,1)} async-done(((bf16[1,32,16,768]{3,2,0,1:T(8,128)(2,1)}), bf16[1,32,16,768]{3,2,0,1:T(8,128)(2,1)}, u32[]{:S(2)}, u32[]{:S(2)}) %all-to-all-start.1) | async-done | bytes 786464 | tf_op jit(solution)/shard_map/while/body/eval_jaxpr/all_to_all | solution.py:179
  271.8 24.0 %all_to_all.26 = bf16[1,32,16,768]{3,2,0,1:T(8,128)(2,1)S(1)} all-to-all(bf16[1,32,16,768]{3,2,0,1:T(8,128)(2,1)S(1)} %bitcast.226), channel_id=1, replica_groups=mesh['fsdp'=32] {'fsdp'}, dimensions={1} | all-to-all | bytes 1572864 | tf_op jit(solution)/shard_map/while/body/eval_jaxpr/all_to_all | solution.py:192
  295.8 18.4 %fusion.149 = (bf16[512,3072]{1,0:T(8,128)(2,1)S(1)}, f32[512,3072]{1,0:T(8,128)}) fusion(f32[3072]{0:T(1024)} %get-tuple-element.567, bf16[512,768]{1,0:T(8,128)(2,1)S(1)} %bitcast.224, bf16[3072,768]{1,0:T(8,128)(2,1)} %get-tuple-element.566), kind=kOutput, calls=%fused_computation.6.clone.1 | convolution fusion | flops 2519728128 | bytes 14954496 | tf_op jit(solution)/shard_map/while/body/eval_jaxpr/dot_general | solution.py:170
  331.3 10.8 %all-to-all-done.1 = bf16[1,32,16,768]{3,2,0,1:T(8,128)(2,1)} async-done(((bf16[1,32,16,768]{3,2,0,1:T(8,128)(2,1)}), bf16[1,32,16,768]{3,2,0,1:T(8,128)(2,1)}, u32[]{:S(2)}, u32[]{:S(2)}) %all-to-all-start.1) | async-done | bytes 786464 | tf_op jit(solution)/shard_map/while/body/eval_jaxpr/all_to_all | solution.py:179
  346.2 134.7 %while.34 = (s32[]{:T(128)}, f32[3072,768]{1,0:T(8,128)}, f32[3072]{0:T(1024)S(1)}, f32[3072,768]{1,0:T(8,128)}, f32[2,1,512,768]{3,2,1,0:T(8,128)}, /*index=5*/...) while((s32[]{:T(128)}, f32[3072,768]{1,0:T(8,128)}, ...), condition=%wide.region_16.18_spmd.clone, body=%wide.region_14.17_spmd.clone.sunk | while | flops 9691204608 | bytes 110936304 | solution.py:248
  362.6 10.2 %all-to-all-done.2 = bf16[1,32,16,768]{3,2,0,1:T(8,128)(2,1)} async-done(((bf16[1,32,16,768]{3,2,0,1:T(8,128)(2,1)}), bf16[1,32,16,768]{3,2,0,1:T(8,128)(2,1)}, u32[]{:S(2)}, u32[]{:S(2)}) %all-to-all-start.2) | async-done | bytes 786464 | tf_op jit(solution)/shard_map/while/body/eval_jaxpr/all_to_all | solution.py:219
  429.9 10.2 %all-to-all-done.2 = bf16[1,32,16,768]{3,2,0,1:T(8,128)(2,1)} async-done(((bf16[1,32,16,768]{3,2,0,1:T(8,128)(2,1)}), bf16[1,32,16,768]{3,2,0,1:T(8,128)(2,1)}, u32[]{:S(2)}, u32[]{:S(2)}) %all-to-all-start.2) | async-done | bytes 786464 | tf_op jit(solution)/shard_map/while/body/eval_jaxpr/all_to_all | solution.py:219
  457.9 11.3 %select_add_fusion.6 = f32[3072,768]{1,0:T(8,128)} fusion(f32[3072,768]{1,0:T(8,128)} %get-tuple-element.585, bf16[512,768]{1,0:T(8,128)(2,1)} %bitcast.227, pred[]{:T(512)S(6)} %compare.4, bf16[512,3072]{1,0:T(8,128)(2,1)} %copy-done.5), kind=kOutput, calls=%fused_computation.37.clone.1 | convolution fusion | flops 2420637696 | bytes 22806528 | tf_op jit(solution)/shard_map/while/body/eval_jaxpr/dot_general | solution.py:235
  480.9 21.4 %gather_fusion.2 = f32[788,768]{1,0:T(8,128)} fusion(f32[2,512,768]{2,1,0:T(8,128)} %bitcast.220, s32[788]{0:T(1024)S(1)} %copy-done.2), kind=kCustom, calls=%fused_computation.1.clone | custom fusion | bytes 4847776 | tf_op jit(solution)/shard_map/vmap(jit(_take))/gather | solution.py:49
  505.9 15.0 %gather_fusion.1 = f32[788,768]{1,0:T(8,128)} fusion(f32[2,512,768]{2,1,0:T(8,128)S(1)} %bitcast.219, s32[788]{0:T(1024)S(1)} %copy-done.2), kind=kCustom, calls=%fused_computation.clone | custom fusion | bytes 4847776 | tf_op jit(solution)/shard_map/vmap(jit(_take))/gather | solution.py:49
  561.3 10.9 %bitcast_convert_fusion.1 = (bf16[2,197,12,64]{1,3,2,0:T(8,128)(2,1)}, f32[2,12,64,197]{3,2,1,0:T(8,128)}) fusion(bf16[2,197,12,64]{1,3,2,0:T(8,128)(2,1)} %bitcast.239, f32[2,12,197,197]{2,3,1,0:T(8,128)} %fusion.96, f32[2,12,197,197]{2,3,1,0:T(8,128)} %copy-done.11, f32[2,12,197]{2,1,0:T(8,128)S(1)} %log.8), kind=kOutput, calls=%fused_computation.92 | convolution fusion | flops 127911504 | bytes 9890976 | tf_op jit(solution)/shard_map/phqk,pkhc->pqhc/dot_general | solution.py:293
  574.4 10.0 %fusion.60 = bf16[2,12,64,197]{3,2,1,0:T(8,128)(2,1)} fusion(bf16[2,197,12,64]{1,3,2,0:T(8,128)(2,1)S(1)} %bitcast.237, f32[2,12,197,197]{2,3,1,0:T(8,128)} %fusion.96, f32[2,12,197,197]{2,3,1,0:T(8,128)} %copy-done.11, f32[2,12,197]{2,1,0:T(8,128)S(1)} %log.8), kind=kOutput, calls=%fused_computation.98 | convolution fusion | flops 127911504 | bytes 8680608 | tf_op jit(solution)/shard_map/phqk,pqhc->pkhc/dot_general | solution.py:296
  608.4 39.6 %all-reduce.17 = (f32[768]{0:T(1024)S(1)}, f32[768]{0:T(1024)S(1)}, f32[768]{0:T(1024)S(1)}, f32[768]{0:T(1024)S(1)}, f32[768]{0:T(1024)S(1)}, /*index=5*/f32[768]{0:T(1024)S(1)}, f32[768]{0:T(1024)S(1)}) all-reduce(f32[768]{0:T(1024)S(1)} %get-tuple-element.293, ...), channel_id=2, replica_groups=mesh['fsdp'=32] {'fsdp'}, use_global_device_ids=true, to_apply=%region_27.29.clone | all-reduce | flops 5376 | bytes 43008
  658.4 77.8 %reduce-scatter.15.cloned.1.call-done = f32[32,24]{0,1:T(8,128)} async-done(((f32[32,768]{0,1:T(8,128)}), f32[32,24]{0,1:T(8,128)}) %reduce-scatter.15.cloned.1.call-update) | async-done | bytes 3088
  736.3 104.4 %reduce-scatter.11.cloned.1.call-done = f32[768,24]{0,1:T(8,128)} async-done(((f32[768,768]{0,1:T(8,128)}), f32[768,24]{0,1:T(8,128)}) %reduce-scatter.11.cloned.1.call-update) | async-done | bytes 73744 | tf_op jit(solution)/shard_map/reduce_scatter | solution.py:332
  840.7 124.7 %reduce-scatter.9.cloned.1.call-done = f32[24,2304]{1,0:T(8,128)} async-done(((f32[768,2304]{1,0:T(8,128)}), f32[24,2304]{1,0:T(8,128)}) %reduce-scatter.9.cloned.1.call-update) | async-done | bytes 221200 | tf_op jit(solution)/shard_map/reduce_scatter | solution.py:329
  (337 shorter events, 268.7 us)
Async XLA Ops:
  7.3 141.5 %all-gather.3.cloned.1.call-start = ((), (), s32[]{:S(2)}) async-start(), calls=%async_computation.8 | async-start | bytes 3649536 | tf_op jit(solution)/shard_map/all_gather | solution.py:101
  8.0 56.1 %copy-start.56 = (bf16[32,24]{0,1:T(8,128)(2,1)S(1)}, bf16[32,24]{0,1:T(8,128)(2,1)}, u32[]{:S(2)}) copy-start(bf16[32,24]{0,1:T(8,128)(2,1)} %param.36) | copy-start | bytes 4612
  8.0 155.5 %all-gather.5.cloned.1.call-start = ((), (), s32[]{:S(2)}) async-start(), calls=%async_computation.9 | async-start | bytes 1216512 | tf_op jit(solution)/shard_map/all_gather | solution.py:104
  8.8 649.7 %reduce-scatter.13.cloned.1.call-start = ((), (), s32[]{:S(2)}) async-start(), calls=%async_computation.12 | async-start | bytes 405504
  12.3 93.3 %copy-start.35 = (bf16[394,768]{1,0:T(8,128)(2,1)S(1)}, bf16[394,768]{1,0:T(8,128)(2,1)}, u32[]{:S(2)}) copy-start(bf16[394,768]{1,0:T(8,128)(2,1)} %param.24) | copy-start | bytes 1815556
  17.5 90.5 %copy-start.57 = (bf16[24,32]{1,0:T(8,128)(2,1)S(1)}, bf16[24,32]{1,0:T(8,128)(2,1)}, u32[]{:S(2)}) copy-start(bf16[24,32]{1,0:T(8,128)(2,1)} %param.35) | copy-start | bytes 4612
  17.8 145.7 %copy-start.12 = (f32[2,197,768]{2,1,0:T(8,128)}, f32[2,197,768]{2,1,0:T(8,128)S(1)}, u32[]{:S(2)}) copy-start(f32[2,197,768]{2,1,0:T(8,128)S(1)} %reshape.390) | copy-start | bytes 3631108
  17.9 134.6 %copy-start.42 = (f32[2,197]{1,0:T(2,128)}, f32[2,197]{1,0:T(2,128)S(1)}, u32[]{:S(2)}) copy-start(f32[2,197]{1,0:T(2,128)S(1)} %div.43) | copy-start | bytes 4732
  62.9 89.6 %copy-start.38 = (f32[768]{0:T(1024)}, f32[768]{0:T(1024)S(1)}, u32[]{:S(2)}) copy-start(f32[768]{0:T(1024)S(1)} %convert_element_type.144) | copy-start | bytes 9220
  62.9 89.6 %copy-start.40 = (f32[768]{0:T(1024)}, f32[768]{0:T(1024)S(1)}, u32[]{:S(2)}) copy-start(f32[768]{0:T(1024)S(1)} %convert_element_type.145) | copy-start | bytes 9220
  63.0 89.5 %copy-start.44 = (f32[2,197]{1,0:T(2,128)}, f32[2,197]{1,0:T(2,128)S(1)}, u32[]{:S(2)}) copy-start(f32[2,197]{1,0:T(2,128)S(1)} %rsqrt.20) | copy-start | bytes 4732
  63.1 104.4 %copy-start.48 = (f32[768]{0:T(1024)}, f32[768]{0:T(1024)S(1)}, u32[]{:S(2)}) copy-start(f32[768]{0:T(1024)S(1)} %convert_element_type.159) | copy-start | bytes 9220
  105.7 88.3 %copy-start.16 = (bf16[2,197,768]{2,1,0:T(8,128)(2,1)}, bf16[2,197,768]{2,1,0:T(8,128)(2,1)S(1)}, u32[]{:S(2)}) copy-start(bf16[2,197,768]{2,1,0:T(8,128)(2,1)S(1)} %reshape.378) | copy-start | bytes 1815556
  244.5 24.3 %all-to-all-start.1 = ((bf16[1,32,16,768]{3,2,0,1:T(8,128)(2,1)}), bf16[1,32,16,768]{3,2,0,1:T(8,128)(2,1)}, u32[]{:S(2)}, u32[]{:S(2)}) async-start(bf16[1,32,16,768]{3,2,0,1:T(8,128)(2,1)} %bitcast.229), calls=%async_computation.1 | async-start | bytes 1572864 | tf_op jit(solution)/shard_map/while/body/eval_jaxpr/all_to_all | solution.py:179
  270.3 44.0 %slice-start = ((s8[4718592]{0:T(1024)(128)(4,1)}), s8[4194304]{0:T(1024)(128)(4,1)S(1)}, s32[]{:S(2)}) async-start(s8[4718592]{0:T(1024)(128)(4,1)} %bitcast.247), calls=%async_computation.14 | async-start | bytes 8388608 | tf_op jit(solution)/shard_map/while
  317.8 24.3 %all-to-all-start.1 = ((bf16[1,32,16,768]{3,2,0,1:T(8,128)(2,1)}), bf16[1,32,16,768]{3,2,0,1:T(8,128)(2,1)}, u32[]{:S(2)}, u32[]{:S(2)}) async-start(bf16[1,32,16,768]{3,2,0,1:T(8,128)(2,1)} %bitcast.229), calls=%async_computation.1 | async-start | bytes 1572864 | tf_op jit(solution)/shard_map/while/body/eval_jaxpr/all_to_all | solution.py:179
  345.6 135.3 %copy-start.2 = (s32[788]{0:T(1024)S(1)}, s32[788]{0:T(1024)}, u32[]{:S(2)}) copy-start(s32[788]{0:T(1024)} %reshape.442) | copy-start | bytes 9460
  348.5 24.3 %all-to-all-start.2 = ((bf16[1,32,16,768]{3,2,0,1:T(8,128)(2,1)}), bf16[1,32,16,768]{3,2,0,1:T(8,128)(2,1)}, u32[]{:S(2)}, u32[]{:S(2)}) async-start(bf16[1,32,16,768]{3,2,0,1:T(8,128)(2,1)} %bitcast.225), calls=%async_computation.2 | async-start | bytes 1572864 | tf_op jit(solution)/shard_map/while/body/eval_jaxpr/all_to_all | solution.py:219
  386.9 24.3 %all-to-all-start.3 = ((bf16[1,32,16,768]{3,2,0,1:T(8,128)(2,1)}), bf16[1,32,16,768]{3,2,0,1:T(8,128)(2,1)}, u32[]{:S(2)}, u32[]{:S(2)}) async-start(bf16[1,32,16,768]{3,2,0,1:T(8,128)(2,1)} %bitcast.228), calls=%async_computation.3 | async-start | bytes 1572864 | tf_op jit(solution)/shard_map/while/body/eval_jaxpr/all_to_all | solution.py:243
  415.8 24.3 %all-to-all-start.2 = ((bf16[1,32,16,768]{3,2,0,1:T(8,128)(2,1)}), bf16[1,32,16,768]{3,2,0,1:T(8,128)(2,1)}, u32[]{:S(2)}, u32[]{:S(2)}) async-start(bf16[1,32,16,768]{3,2,0,1:T(8,128)(2,1)} %bitcast.225), calls=%async_computation.2 | async-start | bytes 1572864 | tf_op jit(solution)/shard_map/while/body/eval_jaxpr/all_to_all | solution.py:219
  454.2 24.3 %all-to-all-start.3 = ((bf16[1,32,16,768]{3,2,0,1:T(8,128)(2,1)}), bf16[1,32,16,768]{3,2,0,1:T(8,128)(2,1)}, u32[]{:S(2)}, u32[]{:S(2)}) async-start(bf16[1,32,16,768]{3,2,0,1:T(8,128)(2,1)} %bitcast.228), calls=%async_computation.3 | async-start | bytes 1572864 | tf_op jit(solution)/shard_map/while/body/eval_jaxpr/all_to_all | solution.py:243
  540.8 195.4 %reduce-scatter.15.cloned.1.call-start = ((), (), s32[]{:S(2)}) async-start(), calls=%async_computation.13 | async-start | bytes 405504
  548.3 292.4 %reduce-scatter.11.cloned.1.call-start = ((), (), s32[]{:S(2)}) async-start(), calls=%async_computation.11 | async-start | bytes 2433024 | tf_op jit(solution)/shard_map/reduce_scatter | solution.py:332
  554.0 411.5 %reduce-scatter.9.cloned.1.call-start = ((), (), s32[]{:S(2)}) async-start(), calls=%async_computation.10 | async-start | bytes 7299072 | tf_op jit(solution)/shard_map/reduce_scatter | solution.py:329
  (61 other events, 456.8 us)
Sparse Core Ops, SparseCore 0:
  11.0 63.4 all-gather.2
  77.4 52.5 all-gather.4
  540.9 95.2 reduce-scatter.12
  641.6 94.6 reduce-scatter.14
  742.0 98.6 reduce-scatter.10
  846.8 118.5 reduce-scatter.8
where the time goes:
time: 980 us; the launch traced here: 972 us
  waiting for transfers between devices  358 us (37%)
  blocking collectives  210 us (21%)
  matrix products  170 us (17%)
  local copies, waits for them, and re-layouts  149 us (15%)
  other arithmetic  47.1 us (5%)
  starting transfers between devices  22.8 us (2%)
  between operations  15.2 us (2%)
    reduce_scatter x1, waiting for transfers between devices, on_device(): lax.psum_scatter(grad_qkv, 'fsdp', scatter_dimension=0, tiled=True)  125 us
    reduce_scatter x1, waiting for transfers between devices, on_device(): lax.psum_scatter(grad_out, 'fsdp', scatter_dimension=1, tiled=True)  104 us
    unnamed x2, blocking collectives  82.2 us
    unnamed x8, waiting for transfers between devices  79.3 us
    all_to_all x2, blocking collectives, forward_group(): lax.all_to_all(outgoing, 'fsdp', split_axis=1, concat_axis=1, tiled=True)  46.5 us
    gather x5, local copies, waits for them, and re-layouts, take_rows(): jnp.take(table_rows, index_rows, axis=0)  44.2 us
    all_gather x1, blocking collectives, on_device(): lax.all_gather(expert_bias, 'fsdp', axis=1, tiled=True)  40.7 us
    all_gather x1, blocking collectives, on_device(): lax.all_gather(w_router, 'fsdp', axis=0, tiled=True)  40.2 us
  transfers between devices with their start and end apart: 12, of which 9 were waited for; matrix products, arithmetic and copies ran while one was open for 18% of the time, Pallas kernels for 0%

commit v1 on v0

v1 whole, which is shorter than its diff:
```python
import math

import jax
import jax.numpy as jnp
from jax import lax
from jax.sharding import PartitionSpec as P

D = 768
HEADS = 12
HEAD_DIM = 64
E = 32
SEQ = 197
CAP = 16
SLOTS = E * CAP
AXIS = "fsdp"
PACK = 3200

epsilon = 1e-06
f32 = jnp.float32
bf16 = jnp.bfloat16


def mm(a, b, ca=1, cb=0):
    return lax.dot_general(a, b, (((ca,), (cb,)), ((), ())), preferred_element_type=f32)


def pieces(v, n):
    out = []
    for _ in range(n):
        p = v.astype(bf16)
        out.append(p)
        v = v - p.astype(f32)
    return out


def mm_split(a, b, n=2, ca=1, cb=0):
    return sum(mm(p, b, ca, cb) for p in pieces(a, n))


def normalize(values):
    centered = values - jnp.mean(values, axis=-1, keepdims=True)
    inverse = lax.rsqrt(jnp.mean(centered * centered, axis=-1, keepdims=True) + epsilon)
    return (centered * inverse, inverse)


def norm_back(upstream, normed, inverse):
    return inverse * (
        upstream
        - jnp.mean(upstream, axis=-1, keepdims=True)
        - normed * jnp.mean(upstream * normed, axis=-1, keepdims=True)
    )


def swap(values, bit):
    n = lax.axis_size(AXIS)
    return lax.ppermute(values, AXIS, [(d, d ^ (1 << bit)) for d in range(n)])


def bit_of(bit):
    return (lax.axis_index(AXIS) >> bit) & 1


def gather_rows(shard):
    bits = lax.axis_size(AXIS).bit_length() - 1
    held = shard[None]
    for bit in reversed(range(bits)):
        theirs = swap(held, bit)
        which = lax.broadcasted_iota(jnp.int32, (1, 2, 1, 1), 1) == bit_of(bit)
        held = jnp.where(which, held[:, None], theirs[:, None])
        held = held.reshape((-1,) + shard.shape)
    return held.reshape((-1,) + shard.shape[1:])


def scatter_rows(rows):
    n = lax.axis_size(AXIS)
    bits = n.bit_length() - 1
    held = rows.reshape((n, rows.shape[0] // n) + rows.shape[1:])
    for bit in range(bits):
        split = held.reshape((held.shape[0] // 2, 2) + held.shape[1:])
        mine = bit_of(bit)
        sent = lax.dynamic_index_in_dim(split, 1 - mine, 1, keepdims=False).astype(bf16)
        kept = lax.dynamic_index_in_dim(split, mine, 1, keepdims=False).astype(f32)
        held = kept + swap(sent, bit).astype(f32)
    return held[0]


def exchange(blocks):
    return lax.all_to_all(blocks, AXIS, split_axis=0, concat_axis=0, tiled=True)


def to_owners(slot_rows, owners):
    rows = slot_rows.reshape((E, 1, CAP) + slot_rows.shape[1:])
    rows = jnp.broadcast_to(rows, (E, owners) + rows.shape[2:])
    return rows.reshape((E * owners, CAP) + slot_rows.shape[1:])


def place(routes):
    ids = jnp.arange(E, dtype=jnp.int32)
    m0 = (routes[:, :1] == ids).astype(bf16)
    m1 = (routes[:, 1:] == ids).astype(bf16)
    t = jnp.arange(SEQ, dtype=jnp.int32)
    lower = (t[None, :] < t[:, None]).astype(bf16)
    c0 = mm(lower, m0)
    c1 = mm(lower, m1) + jnp.sum(m0.astype(f32), axis=0, keepdims=True)
    p0 = jnp.sum(c0 * m0, axis=1, keepdims=True).astype(jnp.int32) + routes[:, :1] * CAP
    p1 = jnp.sum(c1 * m1, axis=1, keepdims=True).astype(jnp.int32) + routes[:, 1:] * CAP
    columns = jnp.arange(SLOTS, dtype=jnp.int32)
    return ((p0 == columns) | (p1 == columns)).astype(bf16), m0 + m1


def gelu_terms(v):
    cumulative = 0.5 * (1.0 + lax.erf(v * (1.0 / math.sqrt(2.0))))
    density = jnp.exp(-0.5 * v * v) * (1.0 / math.sqrt(2.0 * math.pi))
    return v * cumulative, cumulative + v * density


def attend_forward(x, par):
    inputs = x.astype(f32)
    hat1, rstd1 = normalize(inputs)
    norm1 = (hat1 * par["gain1"] + par["shift1"]).astype(bf16)
    proj = mm(norm1, par["qkv"])
    q = (proj[:, :D] + par["bq"]).astype(bf16)
    k = proj[:, D : 2 * D].astype(bf16)
    v = (proj[:, 2 * D :] + par["bv"]).astype(bf16)
    q, k, v = (z.reshape(SEQ, HEADS, HEAD_DIM) for z in (q, k, v))
    scores = jnp.einsum("qhc,khc->hqk", q, k, preferred_element_type=f32) * (
        1.0 / math.sqrt(HEAD_DIM)
    )
    raised = jnp.exp(scores)
    prob = (raised / jnp.sum(raised, axis=-1, keepdims=True)).astype(bf16)
    context = jnp.einsum("hqk,khc->qhc", prob, v, preferred_element_type=f32)
    context = context.astype(bf16).reshape(SEQ, D)
    residual = inputs + mm(context, par["out_t"], 1, 1) + par["bo"]
    hat2, rstd2 = normalize(residual)
    norm2 = (hat2 * par["gain2"] + par["shift2"]).astype(bf16)
    raised2 = jnp.exp(mm(norm2, par["router"]))
    router = raised2 / jnp.sum(raised2, axis=-1, keepdims=True)
    return dict(
        hat1=hat1, rstd1=rstd1, norm1=norm1, q=q, k=k, v=v, prob=prob, context=context,
        residual=residual, hat2=hat2, rstd2=rstd2, norm2=norm2, router=router,
    )


def expert_main(x_rows, c_rows, w_in, w_out, bias_hidden, router_w, expert):
    raised = jnp.exp(mm(x_rows, router_w))
    prob = raised / jnp.sum(raised, axis=-1, keepdims=True)
    picked = jnp.arange(E, dtype=jnp.int32)[None] == expert
    gate = jnp.sum(jnp.where(picked, prob, 0.0), axis=-1, keepdims=True)
    act, slope = gelu_terms(mm(x_rows, w_in, 1, 1) + bias_hidden)
    act = act.astype(bf16)
    hidden = mm(c_rows, w_out, 1, 1)
    gg = jnp.sum(act.astype(f32) * hidden, axis=-1)
    before = hidden * slope * gate
    grad_bias = jnp.sum(before, axis=0)
    before = before.astype(bf16)
    d_rows = mm(before, w_in).astype(bf16)
    gated = (c_rows.astype(f32) * gate).astype(bf16)
    return act, before, gg, grad_bias, d_rows, gated


def token_backward(s, hot, dispatch, slot_grads, gg, cot, par):
    upstream = cot.astype(f32)
    spread = jnp.repeat(jnp.eye(E, dtype=f32), CAP, axis=0) * gg[:, None]
    prob_grad = sum(mm(dispatch, p) for p in pieces(spread, 3))
    prob_grad = prob_grad + mm(cot, par["ebias_t"]) * hot.astype(f32)
    moe_grad = sum(mm(dispatch, rows) for rows in slot_grads)
    router = s["router"]
    logit = router * (prob_grad - jnp.sum(prob_grad * router, axis=-1, keepdims=True))
    logit = logit.astype(bf16)
    g = {}
    g["router"] = mm(s["norm2"], logit, 0, 0)
    second = moe_grad + mm(logit, par["router"], 1, 1)
    g["gain2"] = jnp.sum(second * s["hat2"], axis=0)
    g["shift2"] = jnp.sum(second, axis=0)
    res_grad = upstream + norm_back(second * par["gain2"], s["hat2"], s["rstd2"])
    g["bo"] = jnp.sum(res_grad, axis=0)
    res_half = res_grad.astype(bf16)
    g["out_t"] = mm(res_half, s["context"], 0, 0)
    cg = mm(res_half, par["out_t"]).astype(bf16).reshape(SEQ, HEADS, HEAD_DIM)
    prob = s["prob"]
    vg = jnp.einsum("hqk,qhc->khc", prob, cg, preferred_element_type=f32).reshape(SEQ, D)
    dprob = jnp.einsum("qhc,khc->hqk", cg, s["v"], preferred_element_type=f32)
    pf = prob.astype(f32)
    row_dot = jnp.sum(pf * dprob, axis=-1, keepdims=True)
    sg = (pf * (dprob - row_dot) * (1.0 / math.sqrt(HEAD_DIM))).astype(bf16)
    qg = jnp.einsum("hqk,khc->qhc", sg, s["k"], preferred_element_type=f32).reshape(SEQ, D)
    kg = jnp.einsum("hqk,qhc->khc", sg, s["q"], preferred_element_type=f32).reshape(SEQ, D)
    g["bq"] = jnp.sum(qg, axis=0)
    g["bv"] = jnp.sum(vg, axis=0)
    ph = jnp.concatenate([qg, kg, vg], axis=-1).astype(bf16)
    g["qkv"] = mm(s["norm1"], ph, 0, 0)
    first = mm(ph, par["qkv"], 1, 1)
    g["gain1"] = jnp.sum(first * s["hat1"], axis=0)
    g["shift1"] = jnp.sum(first, axis=0)
    input_grad = res_grad + norm_back(first * par["gain1"], s["hat1"], s["rstd1"])
    weighted = router * hot.astype(f32)
    g["ebias_t"] = sum(mm(cot, p, 0, 0) for p in pieces(weighted, 2))
    return input_grad, g


VECTORS = ("gain1", "shift1", "bq", "bv", "bo", "gain2", "shift2")


def on_device(
    block_in, out_cotangent, expert_routes, ln1_gain, ln1_shift, w_qkv, bias_query, bias_value,
    w_out, bias_out, ln2_gain, ln2_shift, w_router, expert_bias, w_expert_in, bias_hidden,
    w_expert_out,
):
    images = block_in.shape[0] // SEQ
    n = lax.axis_size(AXIS)
    owners = n // E
    expert = lax.axis_index(AXIS) // owners
    own = ln1_gain.shape[0]
    vectors = jnp.stack(
        [ln1_gain, ln1_shift, bias_query, bias_value, bias_out, ln2_gain, ln2_shift], axis=1
    )
    pad = jnp.zeros((own, 128 - 2 * E - len(VECTORS)), bf16)
    shard = jnp.concatenate([w_qkv, w_out.T, w_router, expert_bias.T, vectors, pad], axis=1)
    full = gather_rows(shard)
    small = full[:, 4 * D :]
    rows = small[:, 2 * E : 2 * E + len(VECTORS)].T.astype(f32)
    par = {name: rows[i : i + 1] for i, name in enumerate(VECTORS)}
    par["qkv"] = full[:, : 3 * D]
    par["out_t"] = full[:, 3 * D : 4 * D]
    par["router"] = small[:, :E]
    par["ebias_t"] = small[:, E : 2 * E]

    xs, cots, hots, disp, states, arrived, cot_arrived = [], [], [], [], [], [], []
    for i in range(images):
        xs.append(block_in[i * SEQ : (i + 1) * SEQ])
        cots.append(out_cotangent[i * SEQ : (i + 1) * SEQ])
        d, hot = place(expert_routes[i * SEQ : (i + 1) * SEQ])
        disp.append(d)
        hots.append(hot)
        slots = mm(d, cots[i], 0, 0).astype(bf16)
        cot_arrived.append(exchange(to_owners(slots, owners)).reshape(-1, D))
    for i in range(images):
        states.append(attend_forward(xs[i], par))
        slots = mm(disp[i], states[i]["norm2"], 0, 0).astype(bf16)
        arrived.append(exchange(to_owners(slots, owners)).reshape(-1, D))
    acts, befores, gates, slot_grads, ggs = [], [], [], [], []
    grad_hidden = 0.0
    for i in range(images):
        act, before, gg, gb, d_rows, gated = expert_main(
            arrived[i], cot_arrived[i], w_expert_in, w_expert_out, bias_hidden, par["router"], expert
        )
        acts.append(act)
        befores.append(before)
        gates.append(gated)
        grad_hidden = grad_hidden + gb
        back = exchange(d_rows.reshape(n, CAP, D)).reshape(E, owners, CAP, D)
        slot_grads.append([back[:, o].reshape(SLOTS, D) for o in range(owners)])
        gg_back = exchange(gg.reshape(n, CAP)).reshape(E, owners, CAP)
        ggs.append(jnp.sum(gg_back, axis=1).reshape(SLOTS))
    parts = []
    for i in range(images):
        p = mm(acts[i], w_expert_out).astype(bf16)
        back = exchange(p.reshape(n, CAP, D)).reshape(E, owners, CAP, D)
        parts.append([back[:, o].reshape(SLOTS, D) for o in range(owners)])
    grad_expert_out = sum(mm(acts[i], gates[i], 0, 0) for i in range(images))
    grad_expert_in = sum(mm(befores[i], arrived[i], 0, 0) for i in range(images))

    outs, input_grads, grads = [], [], None
    for i in range(images):
        s = states[i]
        ig, g = token_backward(s, hots[i], disp[i], slot_grads[i], ggs[i], cots[i], par)
        input_grads.append(ig)
        grads = g if grads is None else {k: grads[k] + g[k] for k in g}
    for i in range(images):
        s = states[i]
        gate_hot = s["router"] * hots[i].astype(f32)
        weighted = jnp.repeat(gate_hot, CAP, axis=1) * disp[i].astype(f32)
        moe = mm_split(gate_hot, par["ebias_t"], 2, 1, 1)
        for p in parts[i]:
            moe = moe + mm_split(weighted, p, 2)
        outs.append(s["residual"] + moe)

    vec = jnp.stack([grads[name] for name in VECTORS], axis=1)
    pad = jnp.zeros((D, 128 - 2 * E - len(VECTORS)), f32)
    packed = jnp.concatenate(
        [grads["qkv"], grads["out_t"], grads["router"], grads["ebias_t"], vec, pad], axis=1
    )
    mine = scatter_rows(packed)
    small = mine[:, 4 * D :]
    vec = [small[:, 2 * E + i] for i in range(len(VECTORS))]
    return (
        jnp.concatenate(outs, axis=0),
        jnp.concatenate(input_grads, axis=0),
        vec[0], vec[1], mine[:, : 3 * D], vec[2], vec[3],
        mine[:, 3 * D : 4 * D].T, vec[4], vec[5], vec[6],
        small[:, :E], small[:, E : 2 * E].T,
        grad_expert_in, grad_hidden, grad_expert_out,
    )


def solution(mesh):
    rows, line, cols = P(AXIS, None), P(AXIS), P(None, AXIS)
    in_specs = (
        rows, rows, rows, line, line, rows, line, line, cols, line, line, line, rows, cols,
        rows, line, rows,
    )
    out_specs = (
        rows, rows, line, line, rows, line, line, cols, line, line, line, rows, cols, rows,
        line, rows,
    )
    return jax.shard_map(
        on_device, mesh=mesh, in_specs=in_specs, out_specs=out_specs, check_vma=False
    )
```

time: 980 us -> 483 us (0.49)
  blocking collectives: 210 us -> 0 us
  waiting for transfers between devices: 358 us -> 151 us
  local copies, waits for them, and re-layouts: 149 us -> 61.3 us
  starting transfers between devices: 22.8 us -> 66.9 us
  other arithmetic: 47.1 us -> 21.3 us
  between operations: 15.2 us -> 2.23 us
    reduce_scatter x2 -> x0, waiting for transfers between devices: 229 us -> none  [the longest x1 125 us: on_device(): lax.psum_scatter(grad_qkv, 'fsdp', scatter_dimension=0, tiled=True)]
    ppermute x0 -> x10, waiting for transfers between devices: none -> 87.4 us  [swap(): return lax.ppermute(values, AXIS, [(d, d ^ 1 << bit) for d in range(n)])]
    unnamed x2 -> x0, blocking collectives: 82.2 us -> none
    all_gather x2 -> x0, blocking collectives: 80.9 us -> none  [the longest x1 40.7 us: on_device(): lax.all_gather(expert_bias, 'fsdp', axis=1, tiled=True)]
    unnamed x8 -> x0, waiting for transfers between devices: 79.3 us -> none
    gather x9 -> x0, local copies, waits for them, and re-layouts: 58.2 us -> none  [the longest x5 44.2 us: take_rows(): jnp.take(table_rows, index_rows, axis=0)]
    all_to_all x2 -> x0, blocking collectives: 46.5 us -> none  [forward_group(): lax.all_to_all(outgoing, 'fsdp', split_axis=1, concat_axis=1, tiled=True)]
    all_to_all x6 -> x10, starting transfers between devices: 22.4 us -> 51.7 us  [exchange(): return lax.all_to_all(blocks, AXIS, split_axis=0, concat_axis=0, tiled=True)]
  transfers between devices with their start and end apart: 12 -> 20, of which waited for: 9 -> 14; matrix products, arithmetic and copies ran while one was open for 18% -> 45% of each run, Pallas kernels for 0% -> 0%
where the time goes in v1:
time: 483 us; the launch traced here: 478 us
  matrix products  175 us (36%)
  waiting for transfers between devices  151 us (31%)
  starting transfers between devices  66.9 us (14%)
  local copies, waits for them, and re-layouts  61.3 us (13%)
  other arithmetic  21.3 us (4%)
    dot_general x62, matrix products, mm(): lax.dot_general(a, b, (((ca,), (cb,)), ((), ())), preferred_element_type=...  141 us
    ppermute x10, waiting for transfers between devices, swap(): return lax.ppermute(values, AXIS, [(d, d ^ 1 << bit) for d in range(n)])  87.4 us
    all_to_all x10, waiting for transfers between devices, exchange(): return lax.all_to_all(blocks, AXIS, split_axis=0, concat_axis=0, tiled=True)  63.9 us
    all_to_all x10, starting transfers between devices, exchange(): return lax.all_to_all(blocks, AXIS, split_axis=0, concat_axis=0, tiled=True)  51.7 us
    concatenate x7, local copies, waits for them, and re-layouts, on_device(): jnp.concatenate([grads['qkv'], grads['out_t'], grads['router'], grads['eb...  21.7 us
    ppermute x10, starting transfers between devices, swap(): return lax.ppermute(values, AXIS, [(d, d ^ 1 << bit) for d in range(n)])  15.2 us
    dot_general x2, matrix products, token_backward(): jnp.einsum('hqk,qhc->khc', sg, s['q'], preferred_element_type=f32)  9.85 us
    dot_general x2, matrix products, token_backward(): jnp.einsum('hqk,khc->qhc', sg, s['k'], preferred_element_type=f32)  9.81 us
  transfers between devices with their start and end apart: 20, of which 14 were waited for; matrix products, arithmetic and copies ran while one was open for 45% of the time, Pallas kernels for 0%

profile of v1, /device:TPU:0, one launch (start us, length us, event | category | flops | bytes accessed | tf_op | source)
XLA Modules:
  0.0 477.9 jit_solution(16049167795907743184)
XLA Ops:
  11.0 7.3 %collective-permute-done = bf16[1,24,3200]{2,1,0:T(8,128)(2,1)S(1)} collective-permute-done((bf16[1,24,3200]{2,1,0:T(8,128)(2,1)S(1)}, bf16[1,24,3200]{2,1,0:T(8,128)(2,1)S(1)}, u32[]{:S(2)}, u32[]{:S(2)}) %collective-permute-start) | collective-permute-done | bytes 153632 | tf_op jit(solution)/shard_map/ppermute | solution.py:56
  19.4 7.6 %collective-permute-done.1 = bf16[2,24,3200]{2,1,0:T(8,128)(2,1)S(1)} collective-permute-done((bf16[2,24,3200]{2,1,0:T(8,128)(2,1)S(1)}, bf16[2,24,3200]{2,1,0:T(8,128)(2,1)S(1)}, u32[]{:S(2)}, u32[]{:S(2)}) %collective-permute-start.1) | collective-permute-done | bytes 307232 | tf_op jit(solution)/shard_map/ppermute | solution.py:56
  28.7 12.7 %collective-permute-done.2 = bf16[4,24,3200]{2,1,0:T(8,128)(2,1)S(1)} collective-permute-done((bf16[4,24,3200]{2,1,0:T(8,128)(2,1)S(1)}, bf16[4,24,3200]{2,1,0:T(8,128)(2,1)S(1)}, u32[]{:S(2)}, u32[]{:S(2)}) %collective-permute-start.2) | collective-permute-done | bytes 614432 | tf_op jit(solution)/shard_map/ppermute | solution.py:56
  43.3 25.1 %collective-permute-done.3 = bf16[8,24,3200]{2,1,0:T(8,128)(2,1)S(1)} collective-permute-done((bf16[8,24,3200]{2,1,0:T(8,128)(2,1)S(1)}, bf16[8,24,3200]{2,1,0:T(8,128)(2,1)S(1)}, u32[]{:S(2)}, u32[]{:S(2)}) %collective-permute-start.3) | collective-permute-done | bytes 1228832 | tf_op jit(solution)/shard_map/ppermute | solution.py:56
  73.5 8.7 %all-to-all-start.7 = ((bf16[32,16,768]{2,1,0:T(8,128)(2,1)}), bf16[32,16,768]{2,1,0:T(8,128)(2,1)S(1)}, u32[]{:S(2)}, u32[]{:S(2)}) async-start(bf16[32,16,768]{2,1,0:T(8,128)(2,1)} %bitcast.66), calls=%async_computation.7 | async-start | bytes 1572864 | tf_op jit(solution)/shard_map/all_to_all | solution.py:88
  108.4 5.9 %all-to-all-start = ((bf16[32,16,768]{2,1,0:T(8,128)(2,1)}), bf16[32,16,768]{2,1,0:T(8,128)(2,1)S(1)}, u32[]{:S(2)}, u32[]{:S(2)}) async-start(bf16[32,16,768]{2,1,0:T(8,128)(2,1)} %bitcast.267), calls=%async_computation | async-start | bytes 1572864 | tf_op jit(solution)/shard_map/all_to_all | solution.py:88
  118.3 16.6 %all-to-all-done = bf16[32,16,768]{2,1,0:T(8,128)(2,1)S(1)} async-done(((bf16[32,16,768]{2,1,0:T(8,128)(2,1)}), bf16[32,16,768]{2,1,0:T(8,128)(2,1)S(1)}, u32[]{:S(2)}, u32[]{:S(2)}) %all-to-all-start) | async-done | bytes 786464 | tf_op jit(solution)/shard_map/all_to_all | solution.py:88
  139.6 8.0 %fusion.247 = f32[512,3072]{1,0:T(8,128)} fusion(bf16[512,768]{1,0:T(8,128)(2,1)} %bitcast.270, bf16[3072,768]{1,0:T(8,128)(2,1)} %param.33), kind=kOutput, calls=%fused_computation.407 | convolution fusion | flops 2415919104 | bytes 11796480 | tf_op jit(solution)/shard_map/dot_general | solution.py:24
  151.3 8.8 %all-to-all-done.2 = bf16[32,16,768]{2,1,0:T(8,128)(2,1)S(1)} async-done(((bf16[32,16,768]{2,1,0:T(8,128)(2,1)}), bf16[32,16,768]{2,1,0:T(8,128)(2,1)S(1)}, u32[]{:S(2)}, u32[]{:S(2)}) %all-to-all-start.2) | async-done | bytes 786464 | tf_op jit(solution)/shard_map/all_to_all | solution.py:88
  165.3 7.9 %fusion.244 = f32[512,3072]{1,0:T(8,128)} fusion(bf16[512,768]{1,0:T(8,128)(2,1)} %bitcast.264, bf16[3072,768]{1,0:T(8,128)(2,1)} %param.31), kind=kOutput, calls=%fused_computation.404 | convolution fusion | flops 2415919104 | bytes 11796480 | tf_op jit(solution)/shard_map/dot_general | solution.py:24
  173.2 6.9 %fusion.245 = f32[512,3072]{1,0:T(8,128)} fusion(bf16[512,768]{1,0:T(8,128)(2,1)S(1)} %bitcast.252, bf16[3072,768]{1,0:T(8,128)(2,1)} %param.31), kind=kOutput, calls=%fused_computation.405 | convolution fusion | flops 2415919104 | bytes 11796480 | tf_op jit(solution)/shard_map/dot_general | solution.py:24
  184.5 16.1 %fusion.229 = (f32[3072]{0:T(1024)S(1)}, bf16[512,3072]{1,0:T(8,128)(2,1)}, f32[512]{0:T(512)S(1)}, bf16[512,3072]{1,0:T(8,128)(2,1)}, f32[512]{0:T(512)S(1)}, /...) fusion(f32[512]{0:T(512)S(1)} %get-tuple-element.52, f32[512,3072]{1,0:T(8,128)} %fusion.244, ...), kind=kOutput, calls=%fused_computation.390 | convolution fusion | flops 2472535040 | bytes 37007360 | tf_op jit(solution)/shard_map/dot_general | solution.py:24
  200.6 7.0 %convolution_convert_fusion.2 = bf16[512,768]{1,0:T(8,128)(2,1)} fusion(bf16[512,3072]{1,0:T(8,128)(2,1)S(1)} %get-tuple-element.102, bf16[3072,768]{1,0:T(8,128)(2,1)} %param.33), kind=kOutput, calls=%fused_computation.74 | convolution fusion | flops 2416312320 | bytes 8650752 | tf_op jit(solution)/shard_map/dot_general | solution.py:24
  217.2 5.4 %convolution_add_fusion.1 = f32[3072,768]{1,0:T(8,128)} fusion(f32[3072,768]{1,0:T(8,128)S(1)} %fusion.77, bf16[512,3072]{1,0:T(8,128)(2,1)S(1)} %copy-done.9, bf16[512,768]{1,0:T(8,128)(2,1)S(1)} %bitcast.271, f32[512]{0:T(512)S(1)} %get-tuple-element.53), kind=kOutput, calls=%fused_computation.23 | convolution fusion | flops 2419458048 | bytes 22808576 | tf_op jit(solution)/shard_map/dot_general | solution.py:24
  226.8 5.9 %all-to-all-start.9 = ((f32[32,1,16]{2,1,0:T(1,128)}), f32[32,1,16]{2,1,0:T(1,128)S(1)}, u32[]{:S(2)}, u32[]{:S(2)}) async-start(f32[32,1,16]{2,1,0:T(1,128)} %bitcast.70), calls=%async_computation.9 | async-start | bytes 32768 | tf_op jit(solution)/shard_map/all_to_all | solution.py:88
  232.8 6.8 %fusion.42 = bf16[512,768]{1,0:T(8,128)(2,1)} fusion(bf16[3072,768]{1,0:T(8,128)(2,1)} %param.31, bf16[512,3072]{1,0:T(8,128)(2,1)} %get-tuple-element.57), kind=kOutput, calls=%fused_computation.70 | convolution fusion | flops 2416312320 | bytes 8650752 | tf_op jit(solution)/shard_map/dot_general | solution.py:24
  240.9 5.8 %all-to-all-start.8 = ((bf16[32,16,768]{2,1,0:T(8,128)(2,1)}), bf16[32,16,768]{2,1,0:T(8,128)(2,1)S(1)}, u32[]{:S(2)}, u32[]{:S(2)}) async-start(bf16[32,16,768]{2,1,0:T(8,128)(2,1)} %bitcast.290), calls=%async_computation.8 | async-start | bytes 1572864 | tf_op jit(solution)/shard_map/all_to_all | solution.py:88
  252.6 14.7 %all-to-all-done.8 = bf16[32,16,768]{2,1,0:T(8,128)(2,1)S(1)} async-done(((bf16[32,16,768]{2,1,0:T(8,128)(2,1)}), bf16[32,16,768]{2,1,0:T(8,128)(2,1)S(1)}, u32[]{:S(2)}, u32[]{:S(2)}) %all-to-all-start.8) | async-done | bytes 786464 | tf_op jit(solution)/shard_map/all_to_all | solution.py:88
  281.5 10.2 %all-to-all-done.5 = bf16[32,16,768]{2,1,0:T(8,128)(2,1)} async-done(((bf16[32,16,768]{2,1,0:T(8,128)(2,1)}), bf16[32,16,768]{2,1,0:T(8,128)(2,1)}, u32[]{:S(2)}, u32[]{:S(2)}) %all-to-all-start.5) | async-done | bytes 786464 | tf_op jit(solution)/shard_map/all_to_all | solution.py:88
  361.6 12.7 %concatenate.38 = f32[16,2,24,3200]{3,2,0,1:T(8,128)} concatenate(f32[16,2,24,2304]{3,2,0,1:T(8,128)} %copy.203, f32[16,2,24,768]{3,2,0,1:T(8,128)} %copy.204, f32[16,2,24,32]{3,2,0,1:T(8,128)} %copy.205, f32[16,2,24,32]{3,2,0,1:T(8,128)} %copy.206, f32[16,2,24,1]{3,2,0,1:T(8,128)} %copy.207, f32[16,2,24,1]{3,2,0,1:T(8,128)} %copy.208, f32[16,2,24,1]{3,2,0,1:T(8,128)} %copy.209, ...), dimensions={3} | concatenate | bytes 19660800 | tf_op jit(solution)/shard_map/concatenate | solution.py:280
  395.3 6.0 %all-to-all-start.1 = ((bf16[32,16,768]{2,1,0:T(8,128)(2,1)}), bf16[32,16,768]{2,1,0:T(8,128)(2,1)}, u32[]{:S(2)}, u32[]{:S(2)}) async-start(bf16[32,16,768]{2,1,0:T(8,128)(2,1)} %bitcast.292), calls=%async_computation.1 | async-start | bytes 1572864 | tf_op jit(solution)/shard_map/all_to_all | solution.py:88
  412.6 9.2 %all-to-all-done.1 = bf16[32,16,768]{2,1,0:T(8,128)(2,1)} async-done(((bf16[32,16,768]{2,1,0:T(8,128)(2,1)}), bf16[32,16,768]{2,1,0:T(8,128)(2,1)}, u32[]{:S(2)}, u32[]{:S(2)}) %all-to-all-start.1) | async-done | bytes 786464 | tf_op jit(solution)/shard_map/all_to_all | solution.py:88
  425.6 15.1 %collective-permute-done.6 = bf16[8,24,3200]{2,1,0:T(8,128)(2,1)} collective-permute-done((bf16[8,24,3200]{2,1,0:T(8,128)(2,1)}, bf16[8,24,3200]{2,1,0:T(8,128)(2,1)}, u32[]{:S(2)}, u32[]{:S(2)}) %collective-permute-start.6) | collective-permute-done | bytes 1228832 | tf_op jit(solution)/shard_map/ppermute | solution.py:56
  445.7 12.3 %collective-permute-done.7 = bf16[4,24,3200]{2,1,0:T(8,128)(2,1)S(1)} collective-permute-done((bf16[4,24,3200]{2,1,0:T(8,128)(2,1)S(1)}, bf16[4,24,3200]{2,1,0:T(8,128)(2,1)S(1)}, u32[]{:S(2)}, u32[]{:S(2)}) %collective-permute-start.7) | collective-permute-done | bytes 614432 | tf_op jit(solution)/shard_map/ppermute | solution.py:56
  (345 shorter events, 232.8 us)
Async XLA Ops:
  6.9 11.4 %collective-permute-start = (bf16[1,24,3200]{2,1,0:T(8,128)(2,1)S(1)}, bf16[1,24,3200]{2,1,0:T(8,128)(2,1)S(1)}, u32[]{:S(2)}, u32[]{:S(2)}) collective-permute-start(bf16[1,24,3200]{2,1,0:T(8,128)(2,1)S(1)} %bitcast.293), channel_id=1, source_target_pairs={{0,16},{1,17},{2,18},{3,19},{4,20},{5,21},{6,22},{7,23},{8,24},{9,... | collective-permute-start | bytes 460808 | tf_op jit(solution)/shard_map/ppermute | solution.py:56
  18.5 8.5 %collective-permute-start.1 = (bf16[2,24,3200]{2,1,0:T(8,128)(2,1)S(1)}, bf16[2,24,3200]{2,1,0:T(8,128)(2,1)S(1)}, u32[]{:S(2)}, u32[]{:S(2)}) collective-permute-start(bf16[2,24,3200]{2,1,0:T(8,128)(2,1)S(1)} %broadcast_select_fusion), channel_id=1, source_target_pairs={{0,8},{1,9},{2,10},{3,11},{4,12},{5,13},{6,14},{7,15},{8,0},{9,1},... | collective-permute-start | bytes 921608 | tf_op jit(solution)/shard_map/ppermute | solution.py:56
  27.3 14.2 %collective-permute-start.2 = (bf16[4,24,3200]{2,1,0:T(8,128)(2,1)S(1)}, bf16[4,24,3200]{2,1,0:T(8,128)(2,1)S(1)}, u32[]{:S(2)}, u32[]{:S(2)}) collective-permute-start(bf16[4,24,3200]{2,1,0:T(8,128)(2,1)S(1)} %bitcast_select_fusion.3), channel_id=1, source_target_pairs={{0,4},{1,5},{2,6},{3,7},{4,0},{5,1},{6,2},{7,3},{8,12},{9,13},{10,... | collective-permute-start | bytes 1843208 | tf_op jit(solution)/shard_map/ppermute | solution.py:56
  41.9 26.5 %collective-permute-start.3 = (bf16[8,24,3200]{2,1,0:T(8,128)(2,1)S(1)}, bf16[8,24,3200]{2,1,0:T(8,128)(2,1)S(1)}, u32[]{:S(2)}, u32[]{:S(2)}) collective-permute-start(bf16[8,24,3200]{2,1,0:T(8,128)(2,1)S(1)} %bitcast_select_fusion.2), channel_id=1, source_target_pairs={{0,2},{1,3},{2,0},{3,1},{4,6},{5,7},{6,4},{7,5},{8,10},{9,11},{10,... | collective-permute-start | bytes 3686408 | tf_op jit(solution)/shard_map/ppermute | solution.py:56
  43.3 27.2 %copy-start.44 = (s32[394,2]{0,1:T(2,128)S(1)}, s32[394,2]{0,1:T(2,128)}, u32[]{:S(2)}) copy-start(s32[394,2]{0,1:T(2,128)} %param.19) | copy-start | bytes 9460
  43.3 28.7 %copy-start.23 = (bf16[394,768]{1,0:T(8,128)(2,1)S(1)}, bf16[394,768]{1,0:T(8,128)(2,1)}, u32[]{:S(2)}) copy-start(bf16[394,768]{1,0:T(8,128)(2,1)} %param.18) | copy-start | bytes 1815556
  70.6 12.4 %collective-permute-start.4 = (bf16[16,24,3200]{2,1,0:T(8,128)(2,1)}, bf16[16,24,3200]{2,1,0:T(8,128)(2,1)}, u32[]{:S(2)}, u32[]{:S(2)}) collective-permute-start(bf16[16,24,3200]{2,1,0:T(8,128)(2,1)} %bitcast_select_fusion.1), channel_id=1, source_target_pairs={{0,1},{1,0},{2,3},{3,2},{4,5},{5,4},{6,7},{7,6},{8,9},{9,8},{10,11... | collective-permute-start | bytes 7372808 | tf_op jit(solution)/shard_map/ppermute | solution.py:56
  73.5 34.0 %all-to-all-start.7 = ((bf16[32,16,768]{2,1,0:T(8,128)(2,1)}), bf16[32,16,768]{2,1,0:T(8,128)(2,1)S(1)}, u32[]{:S(2)}, u32[]{:S(2)}) async-start(bf16[32,16,768]{2,1,0:T(8,128)(2,1)} %bitcast.66), calls=%async_computation.7 | async-start | bytes 1572864 | tf_op jit(solution)/shard_map/all_to_all | solution.py:88
  108.4 26.5 %all-to-all-start = ((bf16[32,16,768]{2,1,0:T(8,128)(2,1)}), bf16[32,16,768]{2,1,0:T(8,128)(2,1)S(1)}, u32[]{:S(2)}, u32[]{:S(2)}) async-start(bf16[32,16,768]{2,1,0:T(8,128)(2,1)} %bitcast.267), calls=%async_computation | async-start | bytes 1572864 | tf_op jit(solution)/shard_map/all_to_all | solution.py:88
  135.8 24.4 %all-to-all-start.2 = ((bf16[32,16,768]{2,1,0:T(8,128)(2,1)}), bf16[32,16,768]{2,1,0:T(8,128)(2,1)S(1)}, u32[]{:S(2)}, u32[]{:S(2)}) async-start(bf16[32,16,768]{2,1,0:T(8,128)(2,1)} %bitcast.268), calls=%async_computation.2 | async-start | bytes 1572864 | tf_op jit(solution)/shard_map/all_to_all | solution.py:88
  160.2 24.3 %all-to-all-start.4 = ((bf16[32,16,768]{2,1,0:T(8,128)(2,1)}), bf16[32,16,768]{2,1,0:T(8,128)(2,1)}, u32[]{:S(2)}, u32[]{:S(2)}) async-start(bf16[32,16,768]{2,1,0:T(8,128)(2,1)} %bitcast.291), calls=%async_computation.4 | async-start | bytes 1572864 | tf_op jit(solution)/shard_map/all_to_all | solution.py:88
  208.3 18.6 %all-to-all-start.6 = ((f32[32,1,16]{2,1,0:T(1,128)}), f32[32,1,16]{2,1,0:T(1,128)S(1)}, u32[]{:S(2)}, u32[]{:S(2)}) async-start(f32[32,1,16]{2,1,0:T(1,128)} %bitcast.57), calls=%async_computation.6 | async-start | bytes 32768 | tf_op jit(solution)/shard_map/all_to_all | solution.py:88
  226.8 14.0 %all-to-all-start.9 = ((f32[32,1,16]{2,1,0:T(1,128)}), f32[32,1,16]{2,1,0:T(1,128)S(1)}, u32[]{:S(2)}, u32[]{:S(2)}) async-start(f32[32,1,16]{2,1,0:T(1,128)} %bitcast.70), calls=%async_computation.9 | async-start | bytes 32768 | tf_op jit(solution)/shard_map/all_to_all | solution.py:88
  240.9 26.4 %all-to-all-start.8 = ((bf16[32,16,768]{2,1,0:T(8,128)(2,1)}), bf16[32,16,768]{2,1,0:T(8,128)(2,1)S(1)}, u32[]{:S(2)}, u32[]{:S(2)}) async-start(bf16[32,16,768]{2,1,0:T(8,128)(2,1)} %bitcast.290), calls=%async_computation.8 | async-start | bytes 1572864 | tf_op jit(solution)/shard_map/all_to_all | solution.py:88
  267.3 24.3 %all-to-all-start.5 = ((bf16[32,16,768]{2,1,0:T(8,128)(2,1)}), bf16[32,16,768]{2,1,0:T(8,128)(2,1)}, u32[]{:S(2)}, u32[]{:S(2)}) async-start(bf16[32,16,768]{2,1,0:T(8,128)(2,1)} %bitcast.289), calls=%async_computation.5 | async-start | bytes 1572864 | tf_op jit(solution)/shard_map/all_to_all | solution.py:88
  291.6 103.7 %all-to-all-start.3 = ((bf16[32,16,768]{2,1,0:T(8,128)(2,1)}), bf16[32,16,768]{2,1,0:T(8,128)(2,1)}, u32[]{:S(2)}, u32[]{:S(2)}) async-start(bf16[32,16,768]{2,1,0:T(8,128)(2,1)} %bitcast.288), calls=%async_computation.3 | async-start | bytes 1572864 | tf_op jit(solution)/shard_map/all_to_all | solution.py:88
  378.5 22.8 %collective-permute-start.5 = (bf16[16,24,3200]{2,1,0:T(8,128)(2,1)}, bf16[16,24,3200]{2,1,0:T(8,128)(2,1)}, u32[]{:S(2)}, u32[]{:S(2)}) collective-permute-start(bf16[16,24,3200]{2,1,0:T(8,128)(2,1)} %fusion.18), channel_id=1, source_target_pairs={{0,1},{1,0},{2,3},{3,2},{4,5},{5,4},{6,7},{7,6},{8,9},{9,8},{10,11... | collective-permute-start | bytes 7372808 | tf_op jit(solution)/shard_map/ppermute | solution.py:56
  395.3 26.6 %all-to-all-start.1 = ((bf16[32,16,768]{2,1,0:T(8,128)(2,1)}), bf16[32,16,768]{2,1,0:T(8,128)(2,1)}, u32[]{:S(2)}, u32[]{:S(2)}) async-start(bf16[32,16,768]{2,1,0:T(8,128)(2,1)} %bitcast.292), calls=%async_computation.1 | async-start | bytes 1572864 | tf_op jit(solution)/shard_map/all_to_all | solution.py:88
  408.2 32.4 %collective-permute-start.6 = (bf16[8,24,3200]{2,1,0:T(8,128)(2,1)}, bf16[8,24,3200]{2,1,0:T(8,128)(2,1)}, u32[]{:S(2)}, u32[]{:S(2)}) collective-permute-start(bf16[8,24,3200]{2,1,0:T(8,128)(2,1)} %fusion.58), channel_id=1, source_target_pairs={{0,2},{1,3},{2,0},{3,1},{4,6},{5,7},{6,4},{7,5},{8,10},{9,11},{10,... | collective-permute-start | bytes 3686408 | tf_op jit(solution)/shard_map/ppermute | solution.py:56
  421.9 18.8 %copy-start.2 = (f32[16,24,3200]{2,1,0:T(8,128)S(1)}, f32[16,24,3200]{2,1,0:T(8,128)}, u32[]{:S(2)}) copy-start(f32[16,24,3200]{2,1,0:T(8,128)} %copy-done.1) | copy-start | bytes 14745604
  425.6 18.2 %copy-start.27 = (f32[197,768]{1,0:T(8,128)S(1)}, f32[197,768]{1,0:T(8,128)}, u32[]{:S(2)}) copy-start(f32[197,768]{1,0:T(8,128)} %fusion.168) | copy-start | bytes 1815556
  442.3 15.7 %collective-permute-start.7 = (bf16[4,24,3200]{2,1,0:T(8,128)(2,1)S(1)}, bf16[4,24,3200]{2,1,0:T(8,128)(2,1)S(1)}, u32[]{:S(2)}, u32[]{:S(2)}) collective-permute-start(bf16[4,24,3200]{2,1,0:T(8,128)(2,1)S(1)} %fusion.116), channel_id=1, source_target_pairs={{0,4},{1,5},{2,6},{3,7},{4,0},{5,1},{6,2},{7,3},{8,12},{9,13},{10,... | collective-permute-start | bytes 1843208 | tf_op jit(solution)/shard_map/ppermute | solution.py:56
  458.2 8.3 %collective-permute-start.8 = (bf16[2,24,3200]{2,1,0:T(8,128)(2,1)S(1)}, bf16[2,24,3200]{2,1,0:T(8,128)(2,1)S(1)}, u32[]{:S(2)}, u32[]{:S(2)}) collective-permute-start(bf16[2,24,3200]{2,1,0:T(8,128)(2,1)S(1)} %fusion.132), channel_id=1, source_target_pairs={{0,8},{1,9},{2,10},{3,11},{4,12},{5,13},{6,14},{7,15},{8,0},{9,1},... | collective-permute-start | bytes 921608 | tf_op jit(solution)/shard_map/ppermute | solution.py:56
  466.5 8.3 %collective-permute-start.9 = (bf16[1,24,3200]{2,1,0:T(8,128)(2,1)S(1)}, bf16[1,24,3200]{2,1,0:T(8,128)(2,1)S(1)}, u32[]{:S(2)}, u32[]{:S(2)}) collective-permute-start(bf16[1,24,3200]{2,1,0:T(8,128)(2,1)S(1)} %dynamic-slice_convert_fusion.4), channel_id=1, source_target_pairs={{0,16},{1,17},{2,18},{3,19},{4,20},{5,21},{6,22},{7,23},{8,24},{9,... | collective-permute-start | bytes 460808 | tf_op jit(solution)/shard_map/ppermute | solution.py:56
  (56 other events, 270.9 us)

commit v2 on v1

--- a/solution.py
+++ b/solution.py
@@ -3,6 +3,8 @@
 import jax
 import jax.numpy as jnp
 from jax import lax
+from jax.experimental import pallas as pl
+from jax.experimental.pallas import tpu as pltpu
 from jax.sharding import PartitionSpec as P
 
 D = 768
@@ -141,21 +143,104 @@
     )
 
 
-def expert_main(x_rows, c_rows, w_in, w_out, bias_hidden, router_w, expert):
-    raised = jnp.exp(mm(x_rows, router_w))
-    prob = raised / jnp.sum(raised, axis=-1, keepdims=True)
-    picked = jnp.arange(E, dtype=jnp.int32)[None] == expert
-    gate = jnp.sum(jnp.where(picked, prob, 0.0), axis=-1, keepdims=True)
-    act, slope = gelu_terms(mm(x_rows, w_in, 1, 1) + bias_hidden)
-    act = act.astype(bf16)
-    hidden = mm(c_rows, w_out, 1, 1)
-    gg = jnp.sum(act.astype(f32) * hidden, axis=-1)
-    before = hidden * slope * gate
-    grad_bias = jnp.sum(before, axis=0)
-    before = before.astype(bf16)
-    d_rows = mm(before, w_in).astype(bf16)
-    gated = (c_rows.astype(f32) * gate).astype(bf16)
-    return act, before, gg, grad_bias, d_rows, gated
+def expert_kernel(
+    idx, x, c, w_in, hidden, bias, router, act, back, d_rows, gated, grad_bias, acc, gg, gate
+):
+    r, f = pl.program_id(0), pl.program_id(1)
+    rows, width = act.shape
+
+    @pl.when(f == 0)
+    def _():
+        raised = jnp.exp(mm(x[...], router[...]))
+        picked = lax.broadcasted_iota(jnp.int32, raised.shape, 1) == idx[0]
+        g = jnp.sum(jnp.where(picked, raised, 0.0), axis=1, keepdims=True)
+        g = g / jnp.sum(raised, axis=1, keepdims=True)
+        gate[...] = jnp.broadcast_to(g, gate.shape)
+        gated[...] = (c[...].astype(f32) * g).astype(bf16)
+        gg[...] = jnp.zeros_like(gg)
+        acc[...] = jnp.zeros_like(acc)
+
+    value, slope = gelu_terms(mm(x[...], w_in[...], 1, 1) + bias[...])
+    hid = hidden[...].astype(f32)
+    act[...] = value.astype(bf16)
+    both = value * hid
+    part = both[:, :128]
+    for j in range(1, width // 128):
+        part = part + both[:, j * 128 : (j + 1) * 128]
+    gg[...] += part
+    before = hid * slope * gate[:, :1]
+    total = jnp.sum(before, axis=0, keepdims=True)
+    half = before.astype(bf16)
+    back[...] = half
+    acc[...] += mm(half, w_in[...])
+    cols = pl.ds(pl.multiple_of(f * width, width), width)
+
+    @pl.when(r == 0)
+    def _():
+        grad_bias[:, cols] = total
+
+    @pl.when(r > 0)
+    def _():
+        grad_bias[:, cols] += total
+
+    @pl.when(f == pl.num_programs(1) - 1)
+    def _():
+        d_rows[:, :D] = acc[...].astype(bf16)
+        g = jnp.sum(gg[...], axis=1, keepdims=True)
+        high = g.astype(bf16)
+        low = (g - high.astype(f32)).astype(bf16)
+        lane = lax.broadcasted_iota(jnp.int32, (rows, 128), 1)
+        d_rows[:, D:] = jnp.where(
+            lane == 0,
+            jnp.broadcast_to(high, lane.shape),
+            jnp.where(lane == 1, jnp.broadcast_to(low, lane.shape), jnp.zeros(lane.shape, bf16)),
+        )
+
+
+def expert_main(x, c, w_in, hidden, bias, router, expert):
+    total, width = x.shape[0], w_in.shape[0]
+    rb, fb = min(512, total), min(768, width)
+    row = lambda r, f, *_: (r, 0)
+    tile = lambda r, f, *_: (r, f)
+    fixed = lambda r, f, *_: (0, 0)
+    return pl.pallas_call(
+        expert_kernel,
+        grid_spec=pltpu.PrefetchScalarGridSpec(
+            num_scalar_prefetch=1,
+            grid=(total // rb, width // fb),
+            in_specs=[
+                pl.BlockSpec((rb, D), row),
+                pl.BlockSpec((rb, D), row),
+                pl.BlockSpec((fb, D), lambda r, f, *_: (f, 0)),
+                pl.BlockSpec((rb, fb), tile),
+                pl.BlockSpec((1, fb), lambda r, f, *_: (0, f)),
+                pl.BlockSpec((D, E), fixed),
+            ],
+            out_specs=[
+                pl.BlockSpec((rb, fb), tile),
+                pl.BlockSpec((rb, fb), tile),
+                pl.BlockSpec((rb, D + 128), row),
+                pl.BlockSpec((rb, D), row),
+                pl.BlockSpec((1, width), fixed),
+            ],
+            scratch_shapes=[
+                pltpu.VMEM((rb, D), f32),
+                pltpu.VMEM((rb, 128), f32),
+                pltpu.VMEM((rb, 128), f32),
+            ],
+        ),
+        out_shape=[
+            jax.ShapeDtypeStruct((total, width), bf16),
+            jax.ShapeDtypeStruct((total, width), bf16),
+            jax.ShapeDtypeStruct((total, D + 128), bf16),
+            jax.ShapeDtypeStruct((total, D), bf16),
+            jax.ShapeDtypeStruct((1, width), f32),
+        ],
+        compiler_params=pltpu.CompilerParams(
+            dimension_semantics=("arbitrary", "arbitrary"), vmem_limit_bytes=30 << 20
+        ),
+        name="expert_main",
+    )(expert.reshape(1), x, c, w_in, hidden, bias.reshape(1, width), router)
 
 
 def token_backward(s, hot, dispatch, slot_grads, gg, cot, par):
@@ -225,15 +310,17 @@
     par["router"] = small[:, :E]
     par["ebias_t"] = small[:, E : 2 * E]
 
-    xs, cots, hots, disp, states, arrived, cot_arrived = [], [], [], [], [], [], []
+    xs, cots, hots, disp, states, arrived, outgoing = [], [], [], [], [], [], []
     for i in range(images):
         xs.append(block_in[i * SEQ : (i + 1) * SEQ])
         cots.append(out_cotangent[i * SEQ : (i + 1) * SEQ])
         d, hot = place(expert_routes[i * SEQ : (i + 1) * SEQ])
         disp.append(d)
         hots.append(hot)
-        slots = mm(d, cots[i], 0, 0).astype(bf16)
-        cot_arrived.append(exchange(to_owners(slots, owners)).reshape(-1, D))
+        outgoing.append(to_owners(mm(d, cots[i], 0, 0).astype(bf16), owners))
+    cot_in = exchange(jnp.stack(outgoing, axis=1))
+    cot_rows = [cot_in[:, i].reshape(-1, D) for i in range(images)]
+    hidden = [mm(c, w_expert_out, 1, 1).astype(bf16) for c in cot_rows]
     for i in range(images):
         states.append(attend_forward(xs[i], par))
         slots = mm(disp[i], states[i]["norm2"], 0, 0).astype(bf16)
@@ -241,22 +328,22 @@
     acts, befores, gates, slot_grads, ggs = [], [], [], [], []
     grad_hidden = 0.0
     for i in range(images):
-        act, before, gg, gb, d_rows, gated = expert_main(
-            arrived[i], cot_arrived[i], w_expert_in, w_expert_out, bias_hidden, par["router"], expert
+        act, before, d_rows, gated, gb = expert_main(
+            arrived[i], cot_rows[i], w_expert_in, hidden[i], bias_hidden, par["router"], expert
         )
         acts.append(act)
         befores.append(before)
         gates.append(gated)
-        grad_hidden = grad_hidden + gb
-        back = exchange(d_rows.reshape(n, CAP, D)).reshape(E, owners, CAP, D)
-        slot_grads.append([back[:, o].reshape(SLOTS, D) for o in range(owners)])
-        gg_back = exchange(gg.reshape(n, CAP)).reshape(E, owners, CAP)
-        ggs.append(jnp.sum(gg_back, axis=1).reshape(SLOTS))
-    parts = []
-    for i in range(images):
-        p = mm(acts[i], w_expert_out).astype(bf16)
-        back = exchange(p.reshape(n, CAP, D)).reshape(E, owners, CAP, D)
-        parts.append([back[:, o].reshape(SLOTS, D) for o in range(owners)])
+        grad_hidden = grad_hidden + gb[0]
+        back = exchange(d_rows.reshape(n, CAP, D + 128)).reshape(E, owners, CAP, D + 128)
+        slot_grads.append([back[:, o, :, :D].reshape(SLOTS, D) for o in range(owners)])
+        gg = jnp.sum(back[:, :, :, D : D + 2].astype(f32), axis=(1, 3))
+        ggs.append(gg.reshape(SLOTS))
+    sent = [mm(a, w_expert_out).astype(bf16).reshape(n, CAP, D) for a in acts]
+    back = exchange(jnp.stack(sent, axis=1)).reshape(E, owners, images, CAP, D)
+    parts = [
+        [back[:, o, i].reshape(SLOTS, D) for o in range(owners)] for i in range(images)
+    ]
     grad_expert_out = sum(mm(acts[i], gates[i], 0, 0) for i in range(images))
     grad_expert_in = sum(mm(befores[i], arrived[i], 0, 0) for i in range(images))
 

time: 483 us -> 448 us (0.928)
  matrix products: 175 us -> 136 us
  waiting for transfers between devices: 151 us -> 120 us
  Pallas kernels: 0 us -> 22.7 us
  local copies, waits for them, and re-layouts: 61.3 us -> 83.3 us
  starting transfers between devices: 66.9 us -> 47.2 us
  other arithmetic: 21.3 us -> 29 us
    dot_general x62 -> x56, matrix products: 141 us -> 99.1 us  [mm(): lax.dot_general(a, b, (((ca,), (cb,)), ((), ())), preferred_element_type=...]
    all_to_all x10 -> x6, waiting for transfers between devices: 63.9 us -> 27.9 us  [exchange(): return lax.all_to_all(blocks, AXIS, split_axis=0, concat_axis=0, tiled=True)]
    pallas_call x0 -> x2, Pallas kernels: none -> 22.7 us  [expert_main(): pl.pallas_call(expert_kernel, grid_spec=pltpu.PrefetchScalarGridSpec(num_...]
    all_to_all x10 -> x6, starting transfers between devices: 51.7 us -> 31.9 us  [exchange(): return lax.all_to_all(blocks, AXIS, split_axis=0, concat_axis=0, tiled=True)]
    slice x0 -> x5, local copies, waits for them, and re-layouts: none -> 6.04 us  [the longest x2 2.12 us: on_device(): back[:, o, :, :D].reshape(SLOTS, D)]
    unnamed x120 -> x232, local copies, waits for them, and re-layouts: 5.92 us -> 11.6 us
    slice x4, local copies, waits for them, and re-layouts: 0.4 us -> 5.8 us  [attend_forward(): k = proj[:, D:2 * D].astype(bf16)]
    concatenate x7, local copies, waits for them, and re-layouts: 21.7 us -> 27 us  [on_device(): jnp.concatenate([grads['qkv'], grads['out_t'], grads['router'], grads['eb...]
  transfers between devices with their start and end apart: 20 -> 16, of which waited for: 14 -> 11; matrix products, arithmetic and copies ran while one was open for 45% -> 50% of each run, Pallas kernels for 0% -> 5%
where the time goes in v2:
time: 448 us; the launch traced here: 442 us
  matrix products  136 us (30%)
  waiting for transfers between devices  120 us (27%)
  local copies, waits for them, and re-layouts  83.3 us (19%)
  starting transfers between devices  47.2 us (11%)
  other arithmetic  29 us (6%)
  Pallas kernels  22.7 us (5%)
    dot_general x56, matrix products, mm(): lax.dot_general(a, b, (((ca,), (cb,)), ((), ())), preferred_element_type=...  99.1 us
    ppermute x10, waiting for transfers between devices, swap(): return lax.ppermute(values, AXIS, [(d, d ^ 1 << bit) for d in range(n)])  92.6 us
    all_to_all x6, starting transfers between devices, exchange(): return lax.all_to_all(blocks, AXIS, split_axis=0, concat_axis=0, tiled=True)  31.9 us
    all_to_all x6, waiting for transfers between devices, exchange(): return lax.all_to_all(blocks, AXIS, split_axis=0, concat_axis=0, tiled=True)  27.9 us
    concatenate x7, local copies, waits for them, and re-layouts, on_device(): jnp.concatenate([grads['qkv'], grads['out_t'], grads['router'], grads['eb...  27 us
    pallas_call x2, Pallas kernels, expert_main(): pl.pallas_call(expert_kernel, grid_spec=pltpu.PrefetchScalarGridSpec(num_...  22.7 us
    ppermute x10, starting transfers between devices, swap(): return lax.ppermute(values, AXIS, [(d, d ^ 1 << bit) for d in range(n)])  15.4 us
    unnamed x232, local copies, waits for them, and re-layouts  11.6 us
  transfers between devices with their start and end apart: 16, of which 11 were waited for; matrix products, arithmetic and copies ran while one was open for 50% of the time, Pallas kernels for 5%

profile of v2, /device:TPU:0, one launch (start us, length us, event | category | flops | bytes accessed | tf_op | source)
XLA Modules:
  0.0 441.9 jit_solution(10782249056425738531)
XLA Ops:
  11.1 7.3 %collective-permute-done = bf16[1,24,3200]{2,1,0:T(8,128)(2,1)S(1)} collective-permute-done((bf16[1,24,3200]{2,1,0:T(8,128)(2,1)S(1)}, bf16[1,24,3200]{2,1,0:T(8,128)(2,1)S(1)}, u32[]{:S(2)}, u32[]{:S(2)}) %collective-permute-start) | collective-permute-done | bytes 153632 | tf_op jit(solution)/shard_map/ppermute | solution.py:58
  19.4 7.6 %collective-permute-done.1 = bf16[2,24,3200]{2,1,0:T(8,128)(2,1)S(1)} collective-permute-done((bf16[2,24,3200]{2,1,0:T(8,128)(2,1)S(1)}, bf16[2,24,3200]{2,1,0:T(8,128)(2,1)S(1)}, u32[]{:S(2)}, u32[]{:S(2)}) %collective-permute-start.1) | collective-permute-done | bytes 307232 | tf_op jit(solution)/shard_map/ppermute | solution.py:58
  28.8 12.7 %collective-permute-done.2 = bf16[4,24,3200]{2,1,0:T(8,128)(2,1)S(1)} collective-permute-done((bf16[4,24,3200]{2,1,0:T(8,128)(2,1)S(1)}, bf16[4,24,3200]{2,1,0:T(8,128)(2,1)S(1)}, u32[]{:S(2)}, u32[]{:S(2)}) %collective-permute-start.2) | collective-permute-done | bytes 614432 | tf_op jit(solution)/shard_map/ppermute | solution.py:58
  43.6 24.8 %collective-permute-done.3 = bf16[8,24,3200]{2,1,0:T(8,128)(2,1)S(1)} collective-permute-done((bf16[8,24,3200]{2,1,0:T(8,128)(2,1)S(1)}, bf16[8,24,3200]{2,1,0:T(8,128)(2,1)S(1)}, u32[]{:S(2)}, u32[]{:S(2)}) %collective-permute-start.3) | collective-permute-done | bytes 1228832 | tf_op jit(solution)/shard_map/ppermute | solution.py:58
  74.1 8.3 %all-to-all-start.1 = ((bf16[32,2,16,768]{3,2,1,0:T(8,128)(2,1)}), bf16[32,2,16,768]{3,2,1,0:T(8,128)(2,1)S(1)}, u32[]{:S(2)}, u32[]{:S(2)}) async-start(bf16[32,2,16,768]{3,2,1,0:T(8,128)(2,1)} %pad_maximum_fusion), calls=%async_computation.1 | async-start | bytes 3145728 | tf_op jit(solution)/shard_map/all_to_all | solution.py:90
  113.7 6.4 %all-to-all-done.1 = bf16[32,2,16,768]{3,2,1,0:T(8,128)(2,1)S(1)} async-done(((bf16[32,2,16,768]{3,2,1,0:T(8,128)(2,1)}), bf16[32,2,16,768]{3,2,1,0:T(8,128)(2,1)S(1)}, u32[]{:S(2)}, u32[]{:S(2)}) %all-to-all-start.1) | async-done | bytes 1572896 | tf_op jit(solution)/shard_map/all_to_all | solution.py:90
  125.4 19.1 %all-to-all-done.2 = bf16[32,16,768]{2,1,0:T(8,128)(2,1)S(1)} async-done(((bf16[32,16,768]{2,1,0:T(8,128)(2,1)}), bf16[32,16,768]{2,1,0:T(8,128)(2,1)S(1)}, u32[]{:S(2)}, u32[]{:S(2)}) %all-to-all-start.2) | async-done | bytes 786464 | tf_op jit(solution)/shard_map/all_to_all | solution.py:90
  150.0 5.4 %convolution_convert_fusion.hidden = bf16[512,3072]{1,0:T(8,128)(2,1)S(1)} fusion(bf16[512,768]{1,0:T(8,128)(2,1)S(1)} %bitcast.259, bf16[3072,768]{1,0:T(8,128)(2,1)} %param.33), kind=kOutput, calls=%fused_computation.8 | convolution fusion | flops 2417491968 | bytes 8650752 | tf_op jit(solution)/shard_map/dot_general | solution.py:26
  156.4 11.3 %expert_main.3 = (bf16[512,3072]{1,0:T(8,128)(2,1)S(1)}, bf16[512,3072]{1,0:T(8,128)(2,1)S(1)}, bf16[512,896]{1,0:T(8,128)(2,1)}, bf16[512,768]{1,0:T(8,128)(2,1)S(1)}, f32[1,3072]{1,0:T(1,128)S(1)}) custom-call(s32[1]{0:T(128)} %bitcast.32.idx, bf16[512,768]{1,0:T(8,128)(2,1)S(1)} %bitcast.253, bf16[512,768]{1,0:T(8,128)(2,1)S(1)} %bitcast.260, ...), custom_call_target="tpu_custom_call" | custom-call | tf_op jit(solution)/shard_map/expert_main/pallas_call | solution.py:206
  171.0 6.1 %all-to-all-start.5 = ((bf16[32,16,896]{2,1,0:T(8,128)(2,1)}), bf16[32,16,896]{2,1,0:T(8,128)(2,1)}, u32[]{:S(2)}, u32[]{:S(2)}) async-start(bf16[32,16,896]{2,1,0:T(8,128)(2,1)} %bitcast.77), calls=%async_computation.5 | async-start | bytes 1835008 | tf_op jit(solution)/shard_map/all_to_all | solution.py:90
  177.7 5.4 %convolution_convert_fusion.1.hidden = bf16[512,3072]{1,0:T(8,128)(2,1)S(1)} fusion(bf16[512,768]{1,0:T(8,128)(2,1)S(1)} %bitcast.257, bf16[3072,768]{1,0:T(8,128)(2,1)} %param.33), kind=kOutput, calls=%fused_computation.9 | convolution fusion | flops 2417491968 | bytes 8650752 | tf_op jit(solution)/shard_map/dot_general | solution.py:26
  186.7 11.4 %expert_main.2 = (bf16[512,3072]{1,0:T(8,128)(2,1)S(1)}, bf16[512,3072]{1,0:T(8,128)(2,1)S(1)}, bf16[512,896]{1,0:T(8,128)(2,1)}, bf16[512,768]{1,0:T(8,128)(2,1)S(1)}, f32[1,3072]{1,0:T(1,128)S(1)}) custom-call(s32[1]{0:T(128)} %bitcast.32.idx, bf16[512,768]{1,0:T(8,128)(2,1)S(1)} %bitcast.255, bf16[512,768]{1,0:T(8,128)(2,1)S(1)} %bitcast.258, ...), custom_call_target="tpu_custom_call" | custom-call | tf_op jit(solution)/shard_map/expert_main/pallas_call | solution.py:206
  202.4 5.8 %all-to-all-start.4 = ((bf16[32,16,896]{2,1,0:T(8,128)(2,1)}), bf16[32,16,896]{2,1,0:T(8,128)(2,1)S(1)}, u32[]{:S(2)}, u32[]{:S(2)}) async-start(bf16[32,16,896]{2,1,0:T(8,128)(2,1)} %bitcast.65), calls=%async_computation.4 | async-start | bytes 1835008 | tf_op jit(solution)/shard_map/all_to_all | solution.py:90
  208.2 6.0 %convolution_convert_fusion.2 = bf16[512,768]{1,0:T(8,128)(2,1)S(1)} fusion(bf16[512,3072]{1,0:T(8,128)(2,1)} %copy-done, bf16[3072,768]{1,0:T(8,128)(2,1)} %param.33), kind=kOutput, calls=%fused_computation.45 | convolution fusion | flops 2416312320 | bytes 8650752 | tf_op jit(solution)/shard_map/dot_general | solution.py:26
  214.2 5.0 %convolution_convert_fusion.4 = bf16[512,768]{1,0:T(8,128)(2,1)S(1)} fusion(bf16[512,3072]{1,0:T(8,128)(2,1)S(1)} %copy-done.6, bf16[3072,768]{1,0:T(8,128)(2,1)} %param.33), kind=kOutput, calls=%fused_computation.47 | convolution fusion | flops 2416312320 | bytes 8650752 | tf_op jit(solution)/shard_map/dot_general | solution.py:26
  221.7 5.2 %fusion.191 = f32[3072,768]{1,0:T(8,128)} fusion(bf16[512,3072]{1,0:T(8,128)(2,1)S(1)} %copy-done.9, bf16[512,768]{1,0:T(8,128)(2,1)S(1)} %bitcast.256), kind=kOutput, calls=%fused_computation.348 | convolution fusion | flops 2415919104 | bytes 13369344 | tf_op jit(solution)/shard_map/dot_general | solution.py:26
  267.9 5.5 %fusion.179 = (f32[12,64]{1,0:T(8,128)}, bf16[197,12,64]{0,2,1:T(8,128)(2,1)}) fusion(bf16[197,12,64]{0,2,1:T(8,128)(2,1)} %bitcast.300, bf16[12,197,197]{1,2,0:T(8,128)(2,1)} %copy-done.21, f32[12,197,197]{1,2,0:T(8,128)} %fusion.189), kind=kOutput, calls=%fused_computation.336 | convolution fusion | flops 63174964 | bytes 3402504 | tf_op jit(solution)/shard_map/hqk,khc->qhc/dot_general | solution.py:271
  284.0 4.9 %fusion.31 = bf16[12,64,197]{2,1,0:T(8,128)(2,1)} fusion(bf16[197,12,64]{0,2,1:T(8,128)(2,1)} %bitcast.298, bf16[12,197,197]{1,2,0:T(8,128)(2,1)} %copy-done.20, f32[12,197,197]{1,2,0:T(8,128)} %fusion.188), kind=kOutput, calls=%fused_computation.69 | convolution fusion | flops 63024436 | bytes 3399432 | tf_op jit(solution)/shard_map/hqk,qhc->khc/dot_general | solution.py:272
  288.9 5.5 %fusion.180 = (f32[12,64]{1,0:T(8,128)}, bf16[197,12,64]{0,2,1:T(8,128)(2,1)}) fusion(bf16[197,12,64]{0,2,1:T(8,128)(2,1)} %bitcast.296, bf16[12,197,197]{1,2,0:T(8,128)(2,1)} %copy-done.20, f32[12,197,197]{1,2,0:T(8,128)} %fusion.188), kind=kOutput, calls=%fused_computation.337 | convolution fusion | flops 63174964 | bytes 3402504 | tf_op jit(solution)/shard_map/hqk,khc->qhc/dot_general | solution.py:271
  340.3 12.7 %concatenate.38 = f32[16,2,24,3200]{3,2,0,1:T(8,128)} concatenate(f32[16,2,24,2304]{3,2,0,1:T(8,128)} %copy.193, f32[16,2,24,768]{3,2,0,1:T(8,128)} %copy.194, f32[16,2,24,32]{3,2,0,1:T(8,128)} %copy.195, f32[16,2,24,32]{3,2,0,1:T(8,128)} %copy.196, f32[16,2,24,1]{3,2,0,1:T(8,128)} %copy.197, f32[16,2,24,1]{3,2,0,1:T(8,128)} %copy.198, f32[16,2,24,1]{3,2,0,1:T(8,128)} %copy.199, ...), dimensions={3} | concatenate | bytes 19660800 | tf_op jit(solution)/shard_map/concatenate | solution.py:367
  356.4 7.9 %convolution_add_fusion.2 = f32[3072,768]{1,0:T(8,128)} fusion(f32[3072,768]{1,0:T(8,128)} %fusion.191, bf16[512,3072]{1,0:T(8,128)(2,1)S(1)} %copy-done.3, bf16[512,768]{1,0:T(8,128)(2,1)S(1)} %bitcast.254), kind=kOutput, calls=%fused_computation.4 | convolution fusion | flops 2418278400 | bytes 22806528 | tf_op jit(solution)/shard_map/dot_general | solution.py:26
  367.7 6.0 %convolution_add_fusion.1 = f32[3072,768]{1,0:T(8,128)} fusion(f32[3072,768]{1,0:T(8,128)S(1)} %fusion.192, bf16[512,3072]{1,0:T(8,128)(2,1)S(1)} %copy-done.1, bf16[512,768]{1,0:T(8,128)(2,1)S(1)} %get-tuple-element.35), kind=kOutput, calls=%fused_computation.3 | convolution fusion | flops 2418278400 | bytes 22806528 | tf_op jit(solution)/shard_map/dot_general | solution.py:26
  385.0 20.4 %collective-permute-done.6 = bf16[8,24,3200]{2,1,0:T(8,128)(2,1)} collective-permute-done((bf16[8,24,3200]{2,1,0:T(8,128)(2,1)}, bf16[8,24,3200]{2,1,0:T(8,128)(2,1)}, u32[]{:S(2)}, u32[]{:S(2)}) %collective-permute-start.6) | collective-permute-done | bytes 1228832 | tf_op jit(solution)/shard_map/ppermute | solution.py:58
  410.6 12.4 %collective-permute-done.7 = bf16[4,24,3200]{2,1,0:T(8,128)(2,1)S(1)} collective-permute-done((bf16[4,24,3200]{2,1,0:T(8,128)(2,1)S(1)}, bf16[4,24,3200]{2,1,0:T(8,128)(2,1)S(1)}, u32[]{:S(2)}, u32[]{:S(2)}) %collective-permute-start.7) | collective-permute-done | bytes 614432 | tf_op jit(solution)/shard_map/ppermute | solution.py:58
  (449 shorter events, 216.0 us)
Async XLA Ops:
  0.6 42.7 %copy-start.71 = (s32[394,2]{0,1:T(2,128)S(1)}, s32[394,2]{0,1:T(2,128)}, u32[]{:S(2)}) copy-start(s32[394,2]{0,1:T(2,128)} %param.19) | copy-start | bytes 9460
  6.9 11.4 %collective-permute-start = (bf16[1,24,3200]{2,1,0:T(8,128)(2,1)S(1)}, bf16[1,24,3200]{2,1,0:T(8,128)(2,1)S(1)}, u32[]{:S(2)}, u32[]{:S(2)}) collective-permute-start(bf16[1,24,3200]{2,1,0:T(8,128)(2,1)S(1)} %bitcast.317), channel_id=1, source_target_pairs={{0,16},{1,17},{2,18},{3,19},{4,20},{5,21},{6,22},{7,23},{8,24},{9,... | collective-permute-start | bytes 460808 | tf_op jit(solution)/shard_map/ppermute | solution.py:58
  18.5 8.5 %collective-permute-start.1 = (bf16[2,24,3200]{2,1,0:T(8,128)(2,1)S(1)}, bf16[2,24,3200]{2,1,0:T(8,128)(2,1)S(1)}, u32[]{:S(2)}, u32[]{:S(2)}) collective-permute-start(bf16[2,24,3200]{2,1,0:T(8,128)(2,1)S(1)} %broadcast_select_fusion), channel_id=1, source_target_pairs={{0,8},{1,9},{2,10},{3,11},{4,12},{5,13},{6,14},{7,15},{8,0},{9,1},... | collective-permute-start | bytes 921608 | tf_op jit(solution)/shard_map/ppermute | solution.py:58
  27.3 14.2 %collective-permute-start.2 = (bf16[4,24,3200]{2,1,0:T(8,128)(2,1)S(1)}, bf16[4,24,3200]{2,1,0:T(8,128)(2,1)S(1)}, u32[]{:S(2)}, u32[]{:S(2)}) collective-permute-start(bf16[4,24,3200]{2,1,0:T(8,128)(2,1)S(1)} %bitcast_select_fusion.3), channel_id=1, source_target_pairs={{0,4},{1,5},{2,6},{3,7},{4,0},{5,1},{6,2},{7,3},{8,12},{9,13},{10,... | collective-permute-start | bytes 1843208 | tf_op jit(solution)/shard_map/ppermute | solution.py:58
  41.9 26.5 %collective-permute-start.3 = (bf16[8,24,3200]{2,1,0:T(8,128)(2,1)S(1)}, bf16[8,24,3200]{2,1,0:T(8,128)(2,1)S(1)}, u32[]{:S(2)}, u32[]{:S(2)}) collective-permute-start(bf16[8,24,3200]{2,1,0:T(8,128)(2,1)S(1)} %bitcast_select_fusion.2), channel_id=1, source_target_pairs={{0,2},{1,3},{2,0},{3,1},{4,6},{5,7},{6,4},{7,5},{8,10},{9,11},{10,... | collective-permute-start | bytes 3686408 | tf_op jit(solution)/shard_map/ppermute | solution.py:58
  70.6 12.7 %collective-permute-start.4 = (bf16[16,24,3200]{2,1,0:T(8,128)(2,1)}, bf16[16,24,3200]{2,1,0:T(8,128)(2,1)}, u32[]{:S(2)}, u32[]{:S(2)}) collective-permute-start(bf16[16,24,3200]{2,1,0:T(8,128)(2,1)} %bitcast_select_fusion.1), channel_id=1, source_target_pairs={{0,1},{1,0},{2,3},{3,2},{4,5},{5,4},{6,7},{7,6},{8,9},{9,8},{10,11... | collective-permute-start | bytes 7372808 | tf_op jit(solution)/shard_map/ppermute | solution.py:58
  71.5 40.7 %copy-start.78 = (s32[197,1]{0,1:T(1,128)}, s32[197,1]{0,1:T(1,128)S(1)}, u32[]{:S(2)}) copy-start(s32[197,1]{0,1:T(1,128)S(1)} %get-tuple-element.127) | copy-start | bytes 2368
  71.5 52.3 %copy-start.72 = (s32[197,1]{0,1:T(1,128)}, s32[197,1]{0,1:T(1,128)S(1)}, u32[]{:S(2)}) copy-start(s32[197,1]{0,1:T(1,128)S(1)} %get-tuple-element.125) | copy-start | bytes 2368
  71.5 52.3 %copy-start.75 = (s32[197,1]{0,1:T(1,128)}, s32[197,1]{0,1:T(1,128)S(1)}, u32[]{:S(2)}) copy-start(s32[197,1]{0,1:T(1,128)S(1)} %get-tuple-element.126) | copy-start | bytes 2368
  74.1 46.0 %all-to-all-start.1 = ((bf16[32,2,16,768]{3,2,1,0:T(8,128)(2,1)}), bf16[32,2,16,768]{3,2,1,0:T(8,128)(2,1)S(1)}, u32[]{:S(2)}, u32[]{:S(2)}) async-start(bf16[32,2,16,768]{3,2,1,0:T(8,128)(2,1)} %pad_maximum_fusion), calls=%async_computation.1 | async-start | bytes 3145728 | tf_op jit(solution)/shard_map/all_to_all | solution.py:90
  112.2 32.3 %copy-start.31 = (bf16[197,768]{1,0:T(8,128)(2,1)}, bf16[197,768]{1,0:T(8,128)(2,1)S(1)}, u32[]{:S(2)}) copy-start(bf16[197,768]{1,0:T(8,128)(2,1)S(1)} %get-tuple-element.119) | copy-start | bytes 907780
  120.1 24.4 %all-to-all-start.2 = ((bf16[32,16,768]{2,1,0:T(8,128)(2,1)}), bf16[32,16,768]{2,1,0:T(8,128)(2,1)S(1)}, u32[]{:S(2)}, u32[]{:S(2)}) async-start(bf16[32,16,768]{2,1,0:T(8,128)(2,1)} %bitcast.290), calls=%async_computation.2 | async-start | bytes 1572864 | tf_op jit(solution)/shard_map/all_to_all | solution.py:90
  144.5 26.6 %all-to-all-start = ((bf16[32,16,768]{2,1,0:T(8,128)(2,1)}), bf16[32,16,768]{2,1,0:T(8,128)(2,1)S(1)}, u32[]{:S(2)}, u32[]{:S(2)}) async-start(bf16[32,16,768]{2,1,0:T(8,128)(2,1)} %bitcast.289), calls=%async_computation | async-start | bytes 1572864 | tf_op jit(solution)/shard_map/all_to_all | solution.py:90
  171.0 31.4 %all-to-all-start.5 = ((bf16[32,16,896]{2,1,0:T(8,128)(2,1)}), bf16[32,16,896]{2,1,0:T(8,128)(2,1)}, u32[]{:S(2)}, u32[]{:S(2)}) async-start(bf16[32,16,896]{2,1,0:T(8,128)(2,1)} %bitcast.77), calls=%async_computation.5 | async-start | bytes 1835008 | tf_op jit(solution)/shard_map/all_to_all | solution.py:90
  184.9 57.5 %copy-start.54 = (f32[197,32]{0,1:T(8,128)}, f32[197,32]{0,1:T(8,128)S(1)}, u32[]{:S(2)}) copy-start(f32[197,32]{0,1:T(8,128)S(1)} %get-tuple-element.142) | copy-start | bytes 75652
  186.7 58.6 %copy-start.53 = (f32[197,32]{0,1:T(8,128)}, f32[197,32]{0,1:T(8,128)S(1)}, u32[]{:S(2)}) copy-start(f32[197,32]{0,1:T(8,128)S(1)} %get-tuple-element.146) | copy-start | bytes 75652
  202.4 29.2 %all-to-all-start.4 = ((bf16[32,16,896]{2,1,0:T(8,128)(2,1)}), bf16[32,16,896]{2,1,0:T(8,128)(2,1)S(1)}, u32[]{:S(2)}, u32[]{:S(2)}) async-start(bf16[32,16,896]{2,1,0:T(8,128)(2,1)} %bitcast.65), calls=%async_computation.4 | async-start | bytes 1835008 | tf_op jit(solution)/shard_map/all_to_all | solution.py:90
  231.6 152.0 %all-to-all-start.3 = ((bf16[32,2,16,768]{3,2,1,0:T(8,128)(2,1)}), bf16[32,2,16,768]{3,2,1,0:T(8,128)(2,1)}, u32[]{:S(2)}, u32[]{:S(2)}) async-start(bf16[32,2,16,768]{3,2,1,0:T(8,128)(2,1)} %pad_maximum_fusion.1), calls=%async_computation.3 | async-start | bytes 3145728 | tf_op jit(solution)/shard_map/all_to_all | solution.py:90
  252.1 42.3 %copy-start.22 = (f32[197,768]{1,0:T(8,128)}, f32[197,768]{1,0:T(8,128)S(1)}, u32[]{:S(2)}) copy-start(f32[197,768]{1,0:T(8,128)S(1)} %get-tuple-element.75) | copy-start | bytes 1815556
  355.8 18.0 %collective-permute-start.5 = (bf16[16,24,3200]{2,1,0:T(8,128)(2,1)S(1)}, bf16[16,24,3200]{2,1,0:T(8,128)(2,1)S(1)}, u32[]{:S(2)}, u32[]{:S(2)}) collective-permute-start(bf16[16,24,3200]{2,1,0:T(8,128)(2,1)S(1)} %fusion.6), channel_id=1, source_target_pairs={{0,1},{1,0},{2,3},{3,2},{4,5},{5,4},{6,7},{7,6},{8,9},{9,8},{10,11... | collective-permute-start | bytes 7372808 | tf_op jit(solution)/shard_map/ppermute | solution.py:58
  376.0 29.4 %collective-permute-start.6 = (bf16[8,24,3200]{2,1,0:T(8,128)(2,1)}, bf16[8,24,3200]{2,1,0:T(8,128)(2,1)}, u32[]{:S(2)}, u32[]{:S(2)}) collective-permute-start(bf16[8,24,3200]{2,1,0:T(8,128)(2,1)} %fusion.33), channel_id=1, source_target_pairs={{0,2},{1,3},{2,0},{3,1},{4,6},{5,7},{6,4},{7,5},{8,10},{9,11},{10,... | collective-permute-start | bytes 3686408 | tf_op jit(solution)/shard_map/ppermute | solution.py:58
  407.8 15.2 %collective-permute-start.7 = (bf16[4,24,3200]{2,1,0:T(8,128)(2,1)S(1)}, bf16[4,24,3200]{2,1,0:T(8,128)(2,1)S(1)}, u32[]{:S(2)}, u32[]{:S(2)}) collective-permute-start(bf16[4,24,3200]{2,1,0:T(8,128)(2,1)S(1)} %fusion.82), channel_id=1, source_target_pairs={{0,4},{1,5},{2,6},{3,7},{4,0},{5,1},{6,2},{7,3},{8,12},{9,13},{10,... | collective-permute-start | bytes 1843208 | tf_op jit(solution)/shard_map/ppermute | solution.py:58
  423.1 7.7 %collective-permute-start.8 = (bf16[2,24,3200]{2,1,0:T(8,128)(2,1)S(1)}, bf16[2,24,3200]{2,1,0:T(8,128)(2,1)S(1)}, u32[]{:S(2)}, u32[]{:S(2)}) collective-permute-start(bf16[2,24,3200]{2,1,0:T(8,128)(2,1)S(1)} %fusion.96), channel_id=1, source_target_pairs={{0,8},{1,9},{2,10},{3,11},{4,12},{5,13},{6,14},{7,15},{8,0},{9,1},... | collective-permute-start | bytes 921608 | tf_op jit(solution)/shard_map/ppermute | solution.py:58
  430.9 7.8 %collective-permute-start.9 = (bf16[1,24,3200]{2,1,0:T(8,128)(2,1)S(1)}, bf16[1,24,3200]{2,1,0:T(8,128)(2,1)S(1)}, u32[]{:S(2)}, u32[]{:S(2)}) collective-permute-start(bf16[1,24,3200]{2,1,0:T(8,128)(2,1)S(1)} %dynamic-slice_convert_fusion.4), channel_id=1, source_target_pairs={{0,16},{1,17},{2,18},{3,19},{4,20},{5,21},{6,22},{7,23},{8,24},{9,... | collective-permute-start | bytes 460808 | tf_op jit(solution)/shard_map/ppermute | solution.py:58
  (108 other events, 704.5 us)
